TPU v7x, 256 devices: a whole 4x4x8 slice. The times are simulated.
256 devices in a mesh: gx: 16 (over z_lo, y), gy: 4 (over x), gz: 4 (over z_hi, core).
Axes of the slice: x: 4, y: 4, z: 8 (z_hi: 2, z_lo: 4; z = z_hi * 4 + z_lo), core: 2. Of those that a mesh axis runs over, the one named last changes fastest.
Arguments:
- saved_thermal_values: float32 [256, 128, 1024], P('gx', 'gy', 'gz'), may hold values from -4 to 4
- saved_transformed_share: float32 [256, 128, 1024], P('gx', 'gy', 'gz'), may hold values from 0 to 0.9
- diffusion_numbers: float32 [256, 128, 1024], P('gx', 'gy', 'gz'), may hold values from 0.04 to 0.15
- transformation_status: int32 [256, 128, 1024], P('gx', 'gy', 'gz'), may hold values from 0 to 2
- boundary_conductances: float32 [1835008], P(('gx', 'gy', 'gz')), may hold values from 0.02 to 0.2
- boundary_voxel_locator: int32 [524288], P(('gx', 'gy', 'gz')), may hold values from 0 to 131071, as said below
- boundary_conductance_locator: int32 [524288], P(('gx', 'gy', 'gz')), may hold values from 0 to 1835007, as said below
- boundary_patch_extent: float32 [524288], P(('gx', 'gy', 'gz')), may hold values from 0.5 to 1.5
- boundary_active_entries: int32 [256], P(('gx', 'gy', 'gz')), may hold values from 1024 to 2048, as said below
- thermal_error_factor: float32 [256, 128, 1024], P('gx', 'gy', 'gz'), may hold values from -6 to 6
- product_error_factor: float32 [256, 128, 1024], P('gx', 'gy', 'gz'), may hold values from -6 to 6
Outputs:
- temp_final: float32 [256, 128, 1024], P('gx', 'gy', 'gz')
- phase_final: float32 [256, 128, 1024], P('gx', 'gy', 'gz')
- transfer_sensitivity: float32 [1835008], P(('gx', 'gy', 'gz'))
Inputs may be any that keep to these rules, and one draw needn't show every extreme that they name: `boundary_voxel_locator`: within each brick's 2048 slots (aligned blocks of the array), the cell indices are distinct and increasing. `boundary_conductance_locator`: A slot of a brick whose gx index is i names a coefficient in [i * 114688, (i + 1) * 114688). `boundary_active_entries`: entry d is the number of live leading slots of brick d (flat over gx, gy, gz); the others are empty. Some brick has all 2048 slots live.
All inputs are finite; a program needn't handle non-finite values.
Results may differ from a plain program's by a relative error of at most 0.00002.
Values sent between devices are 32-bit elements; how exact they have to be, the bound alone decides.
A program may use at most 64 MiB of HBM per device.

v0:
```python
import jax
import jax.numpy as jnp
from jax import lax
from jax.sharding import PartitionSpec as P

sharpness = 4.0
onset_temp = 0.0
kinetic_fast = 0.6
kinetic_slow = 0.2
enthalpy_release = 0.4
bath_thermal_level = -2.0


def padded_2(x, sides, width):
    for axis, dim in sides:
        peers, length = (lax.axis_size(axis), x.shape[dim])
        up = [(i, (i + 1) % peers) for i in range(peers - 1)]
        down = [(j, i) for i, j in up]
        last = lax.slice_in_dim(x, length - width, length, axis=dim)
        leading = lax.slice_in_dim(x, 0, width, axis=dim)
        before = lax.ppermute(last, axis, up)
        after = lax.ppermute(leading, axis, down)
        x = jnp.concatenate([before, x, after], axis=dim)
    return x


def copy_for_each(x, axis):
    copies = jnp.broadcast_to(x, (lax.axis_size(axis), *x.shape))
    return lax.all_to_all(copies, axis, split_axis=0, concat_axis=0, tiled=True)


def in_order(parts, dim):
    parts = jnp.moveaxis(parts, 0, dim)
    lengths = parts.shape
    return parts.reshape(*lengths[:dim], lengths[dim] * lengths[dim + 1], *lengths[dim + 2 :])


def collect(x, axis, dim):
    parts = copy_for_each(x, axis)
    return in_order(parts, dim)


def extended(x, sides, width):
    edges = {}
    for axis, dim in sides:
        peers, length = (lax.axis_size(axis), x.shape[dim])
        up = [(i, (i + 1) % peers) for i in range(peers - 1)]
        last = lax.slice_in_dim(x, length - width, length, axis=dim)
        leading = lax.slice_in_dim(x, 0, width, axis=dim)
        edges[dim] = (
            lax.ppermute(last, axis, up),
            lax.ppermute(leading, axis, [(b, a) for a, b in up]),
        )
    done = []
    for _, dim in sides:
        low, high = edges[dim]
        around = [(width, width) if d in done else (0, 0) for d in range(x.ndim)]
        x = jnp.concatenate([jnp.pad(low, around), x, jnp.pad(high, around)], axis=dim)
        done.append(dim)
    return x


def cut_along(x, dim, peers):
    before, after = (x.shape[:dim], x.shape[dim + 1 :])
    return jnp.moveaxis(x.reshape(*before, peers, -1, *after), dim, 0)


def summed_on_arrival(x, axis, dim):
    parts = cut_along(x, dim, lax.axis_size(axis))
    arrived = lax.all_to_all(parts, axis, split_axis=0, concat_axis=0, tiled=True)
    return arrived.sum(axis=0)


def adjacent_values(padded):
    total = padded[2:, 1:-1, 1:-1] + padded[:-2, 1:-1, 1:-1]
    total = total + padded[1:-1, 2:, 1:-1] + padded[1:-1, :-2, 1:-1]
    total = total + padded[1:-1, 1:-1, 2:] + padded[1:-1, 1:-1, :-2]
    return total


def march_forward_once(
    padded,
    present_thermal_values,
    frac_now,
    diffusion_numbers,
    transformation_speed,
    thermal_drain_grid,
):
    gate_value = jax.nn.sigmoid(sharpness * (onset_temp - present_thermal_values))
    product_increase = transformation_speed * (1.0 - frac_now) * gate_value
    new_frac = frac_now + product_increase
    updated_thermal_values = (
        present_thermal_values
        + diffusion_numbers * (adjacent_values(padded) - 6.0 * present_thermal_values)
        + enthalpy_release * product_increase
        - thermal_drain_grid * (present_thermal_values - bath_thermal_level)
    )
    return (updated_thermal_values, new_frac, gate_value)


def on_device(
    saved_thermal_values,
    saved_transformed_share,
    diffusion_numbers,
    transformation_status,
    boundary_conductances,
    boundary_voxel_locator,
    boundary_conductance_locator,
    boundary_patch_extent,
    boundary_active_entries,
    thermal_error_factor,
    product_error_factor,
):
    subdomain_extents = saved_thermal_values.shape
    total_voxels = saved_thermal_values.size
    slot_count = boundary_voxel_locator.shape[0]
    scaled_cotangent = diffusion_numbers * thermal_error_factor
    stacked = padded_2(
        jnp.stack([saved_thermal_values, scaled_cotangent]), (("gx", 1), ("gy", 2), ("gz", 3)), 1
    )
    front_bordered_grid = stacked[0]
    carried = stacked[1]
    transformation_speed = kinetic_fast * (transformation_status == 1).astype(
        jnp.float32
    ) + kinetic_slow * (transformation_status == 2).astype(jnp.float32)
    alive_slot = (jnp.arange(slot_count, dtype=jnp.int32) < boundary_active_entries[0]).astype(
        jnp.float32
    )
    weight = alive_slot * boundary_patch_extent
    coef_slab = collect(boundary_conductances, ("gy", "gz"), 0)
    slab_start = lax.axis_index("gx") * coef_slab.shape[0]
    values = coef_slab[boundary_conductance_locator - slab_start]
    thermal_drain_grid = (
        jnp.zeros((total_voxels,), jnp.float32)
        .at[boundary_voxel_locator]
        .set(weight * values)
        .reshape(subdomain_extents)
    )
    thermal_values_next, transformed_share_next, primary_switch = march_forward_once(
        front_bordered_grid,
        saved_thermal_values,
        saved_transformed_share,
        diffusion_numbers,
        transformation_speed,
        thermal_drain_grid,
    )
    another_bordered_grid = extended(thermal_values_next, (("gx", 0), ("gy", 1), ("gz", 2)), 1)
    temp_two, frac_two, gate_value = march_forward_once(
        another_bordered_grid,
        thermal_values_next,
        transformed_share_next,
        diffusion_numbers,
        transformation_speed,
        thermal_drain_grid,
    )
    increase_derivative = (
        transformation_speed
        * (1.0 - transformed_share_next)
        * gate_value
        * (1.0 - gate_value)
        * -sharpness
    )
    dual_thermal_values = (
        thermal_error_factor * (1.0 - 6.0 * diffusion_numbers - thermal_drain_grid)
        + adjacent_values(carried)
        + (enthalpy_release * thermal_error_factor + product_error_factor) * increase_derivative
    )
    heat_sink_gradient = -(
        thermal_error_factor * (thermal_values_next - bath_thermal_level)
        + dual_thermal_values * (saved_thermal_values - bath_thermal_level)
    )
    slot_grad = weight * heat_sink_gradient.reshape(-1)[boundary_voxel_locator]
    spread = (
        jnp.zeros((coef_slab.shape[0],), jnp.float32)
        .at[boundary_conductance_locator - slab_start]
        .add(slot_grad)
    )
    transfer_sensitivity = summed_on_arrival(spread, ("gy", "gz"), 0)
    return (temp_two, frac_two, transfer_sensitivity)


def solution(mesh):
    in_specs = (
        P("gx", "gy", "gz"),
        P("gx", "gy", "gz"),
        P("gx", "gy", "gz"),
        P("gx", "gy", "gz"),
        P(("gx", "gy", "gz")),
        P(("gx", "gy", "gz")),
        P(("gx", "gy", "gz")),
        P(("gx", "gy", "gz")),
        P(("gx", "gy", "gz")),
        P("gx", "gy", "gz"),
        P("gx", "gy", "gz"),
    )
    out_specs = (P("gx", "gy", "gz"), P("gx", "gy", "gz"), P(("gx", "gy", "gz")))
    return jax.shard_map(
        on_device, mesh=mesh, in_specs=in_specs, out_specs=out_specs, check_vma=False
    )
```

profile of v0, /device:TPU:32, one launch (start us, length us, event | category | flops | bytes accessed | tf_op | source)
XLA Modules:
  0.0 143.2 jit_solution(11764988883190933123)
XLA Ops:
  0.6 1.3 multiply_bitcast_fusion
  2.0 0.0 copy-done
  2.0 0.0 copy-start.9
  2.0 3.5 %collective-permute-start = (f32[2,1,32,256]{3,2,1,0:T(8,128)S(1)}, f32[2,1,32,256]{3,2,1,0:T(8,128)S(1)}, u32[]{:S(2)}, u32[]{:S(2)}) collective-permute-start(f32[2,1,32,256]{3,2,1,0:T(8,128)S(1)} %get-tuple-element.18), channel_id=1, source_target_pairs={{0,16},{16,32},{32,48},{48,64},{64,80},{80,96},{96,112},{112,128},... | collective-permute-start | bytes 196616 | tf_op jit(solution)/shard_map/ppermute | solution.py:21
  5.5 4.5 %collective-permute-start.1 = (f32[2,1,32,256]{3,2,1,0:T(8,128)S(1)}, f32[2,1,32,256]{3,2,1,0:T(8,128)S(1)}, u32[]{:S(2)}, u32[]{:S(2)}) collective-permute-start(f32[2,1,32,256]{3,2,1,0:T(8,128)S(1)} %get-tuple-element.19), channel_id=1, source_target_pairs={{16,0},{32,16},{48,32},{64,48},{80,64},{96,80},{112,96},{128,112},... | collective-permute-start | bytes 196616 | tf_op jit(solution)/shard_map/ppermute | solution.py:22
  10.0 1.0 broadcast_in_dim.19
  11.0 10.1 %all-to-all-start = ((f32[16,1,7168]{2,1,0:T(1,128)}), f32[16,1,7168]{2,1,0:T(1,128)S(1)}, u32[]{:S(2)}, u32[]{:S(2)}) async-start(f32[16,1,7168]{2,1,0:T(1,128)} %broadcast_in_dim.19), calls=%async_computation | async-start | bytes 917504 | tf_op jit(solution)/shard_map/all_to_all | solution.py:29
  21.1 0.0 collective-permute-done
  21.2 0.0 collective-permute-done.1
  21.2 0.1 pad_maximum_fusion.23
  21.2 3.8 %collective-permute-start.2 = (f32[2,18,1,256]{3,2,1,0:T(1,128)S(1)}, f32[2,18,1,256]{3,2,1,0:T(1,128)S(1)}, u32[]{:S(2)}, u32[]{:S(2)}) collective-permute-start(f32[2,18,1,256]{3,2,1,0:T(1,128)S(1)} %get-tuple-element.16), channel_id=1, source_target_pairs={{0,4},{4,8},{8,12},{1,5},{5,9},{9,13},{2,6},{6,10},{10,14},{3,7},{... | collective-permute-start | bytes 110600 | tf_op jit(solution)/shard_map/ppermute | solution.py:21
  25.1 1.3 collective-permute-start.3
  26.4 0.3 collective-permute-done.2
  26.7 4.2 %collective-permute-done.3 = f32[2,18,1,256]{3,2,1,0:T(1,128)S(1)} collective-permute-done((f32[2,18,1,256]{3,2,1,0:T(1,128)S(1)}, f32[2,18,1,256]{3,2,1,0:T(1,128)S(1)}, u32[]{:S(2)}, u32[]{:S(2)}) %collective-permute-start.3) | collective-permute-done | bytes 36896 | tf_op jit(solution)/shard_map/ppermute | solution.py:22
  30.9 0.2 pad_maximum_fusion.1
  31.1 0.3 fusion.30
  31.4 0.3 copy.43
  31.7 1.3 collective-permute-start.4
  33.0 0.3 copy.44
  33.4 1.3 collective-permute-start.5
  34.7 0.6 broadcast_clamp_fusion.1
  35.9 0.0 collective-permute-done.4
  35.9 0.4 copy.45
  36.3 5.7 %collective-permute-done.5 = f32[2,18,34,1]{2,0,3,1:T(2,128)S(1)} collective-permute-done((f32[2,18,34,1]{2,0,3,1:T(2,128)S(1)}, f32[2,18,34,1]{2,0,3,1:T(2,128)S(1)}, u32[]{:S(2)}, u32[]{:S(2)}) %collective-permute-start.5) | collective-permute-done | bytes 4928 | tf_op jit(solution)/shard_map/ppermute | solution.py:22
  42.1 0.4 copy.46
  42.4 1.1 pad_maximum_fusion
  43.6 0.1 slice_bitcast_fusion.1
  43.7 0.0 all-to-all-done
  43.7 0.0 copy-start.7
  43.8 11.8 %gather_fusion = f32[2048]{0:T(1024)S(1)} fusion(f32[114688]{0:T(1024)S(1)} %bitcast.14, s32[2048]{0:T(1024)S(1)} %get-tuple-element.10), kind=kCustom, calls=%fused_computation | custom fusion | bytes 24576 | tf_op jit(solution)/shard_map/gather | solution.py:132
  55.5 0.0 copy-start.3
  55.6 0.0 copy-done.7
  55.6 8.8 %scatter_custom_fusion = f32[131072]{0:T(1024)} fusion(s32[2048]{0:T(1024)S(1)} %get-tuple-element.27, f32[2048]{0:T(1024)S(1)} %fusion.28, f32[]{:T(128)} %constant.19.clone.1), kind=kCustom, calls=%fused_computation.65 | custom fusion | bytes 524292 | tf_op jit(solution)/shard_map/scatter | solution.py:136
  64.4 2.0 %reshape.25 = f32[16,32,256]{2,1,0:T(8,128)} reshape(f32[131072]{0:T(1024)} %scatter_custom_fusion) | data formatting | bytes 1048576 | tf_op jit(solution)/shard_map/reshape | solution.py:137
  66.4 0.0 copy-done.3
  66.4 3.4 %fusion.4 = (f32[16,32,256]{2,1,0:T(8,128)S(1)}, f32[16,32,256]{2,1,0:T(8,128)S(1)}, pred[16,32,256]{2,1,0:T(8,128)(4,1)S(1)}, pred[16,32,256]{2,1,0:T(8,128)(4,1)S(1)}) fusion(f32[18,34,258]{2,1,0:T(8,128)S(1)} %get-tuple-element.13, f32[16,32,256]{2,1,0:T(8,128)} %param.21, f32[16,32,256]{2,1,0:T(8,128)} %param.20, f32[16,32,256]{2,1,0:T(8,128)} %reshape.25, ...), kind=kLoop, calls=%fused_computation.13 | loop fusion | flops 7602176 | bytes 11272192 | tf_op jit(solution)/shard_map/neg | solution.py:168
  69.8 0.0 copy-start.1
  69.8 1.0 fusion.31
  70.8 1.3 collective-permute-start.10
  72.1 9.6 %collective-permute-start.11 = (f32[16,32,1]{2,1,0:T(8,128)}, f32[16,32,1]{2,1,0:T(8,128)}, u32[]{:S(2)}, u32[]{:S(2)}) collective-permute-start(f32[16,32,1]{2,1,0:T(8,128)} %get-tuple-element.21), channel_id=1, source_target_pairs={{0,1},{1,2},{2,3},{4,5},{5,6},{6,7},{8,9},{9,10},{10,11},{12,13},{... | collective-permute-start | bytes 6152 | tf_op jit(solution)/shard_map/ppermute | solution.py:51
  81.7 3.2 %collective-permute-start.6 = (f32[1,32,256]{2,1,0:T(8,128)S(1)}, f32[1,32,256]{2,1,0:T(8,128)S(1)}, u32[]{:S(2)}, u32[]{:S(2)}) collective-permute-start(f32[1,32,256]{2,1,0:T(8,128)S(1)} %get-tuple-element.23), channel_id=1, source_target_pairs={{16,0},{32,16},{48,32},{64,48},{80,64},{96,80},{112,96},{128,112},... | collective-permute-start | bytes 98312 | tf_op jit(solution)/shard_map/ppermute | solution.py:52
  85.0 2.6 %collective-permute-start.7 = (f32[1,32,256]{2,1,0:T(8,128)S(1)}, f32[1,32,256]{2,1,0:T(8,128)S(1)}, u32[]{:S(2)}, u32[]{:S(2)}) collective-permute-start(f32[1,32,256]{2,1,0:T(8,128)S(1)} %get-tuple-element.22), channel_id=1, source_target_pairs={{0,16},{16,32},{32,48},{48,64},{64,80},{80,96},{96,112},{112,128},... | collective-permute-start | bytes 98312 | tf_op jit(solution)/shard_map/ppermute | solution.py:51
  87.6 1.3 collective-permute-start.8
  88.9 0.0 copy-done.1
  88.9 0.3 copy.49
  89.2 11.8 %gather_fusion.1 = f32[2048]{0:T(1024)S(1)} fusion(f32[131072]{0:T(1024)S(1)} %bitcast.15, s32[2048]{0:T(1024)S(1)} %get-tuple-element.26), kind=kCustom, calls=%fused_computation.1 | custom fusion | bytes 24576 | tf_op jit(solution)/shard_map/gather | solution.py:172
  101.0 0.0 copy-start.2
  101.0 0.0 copy-start.6
  101.0 12.3 %scatter_custom_fusion.1 = f32[114688]{0:T(1024)} fusion(s32[2048]{0:T(1024)} %get-tuple-element.11, f32[2048]{0:T(1024)S(1)} %fusion.27, f32[]{:T(128)} %constant.19.clone.1), kind=kCustom, calls=%fused_computation.70 | custom fusion | flops 2048 | bytes 459264 | tf_op jit(solution)/shard_map/scatter-add | solution.py:176
  113.3 10.1 %all-to-all-start.1 = ((f32[16,1,7168]{2,1,0:T(1,128)}), f32[16,1,7168]{2,1,0:T(1,128)S(1)}, u32[]{:S(2)}, u32[]{:S(2)}) async-start(f32[16,1,7168]{2,1,0:T(1,128)} %bitcast.6), calls=%async_computation.1 | async-start | bytes 917504 | tf_op jit(solution)/shard_map/all_to_all | solution.py:70
  123.4 0.0 collective-permute-done.8
  123.4 3.8 %collective-permute-start.9 = (f32[16,1,256]{2,1,0:T(1,128)S(1)}, f32[16,1,256]{2,1,0:T(1,128)S(1)}, u32[]{:S(2)}, u32[]{:S(2)}) collective-permute-start(f32[16,1,256]{2,1,0:T(1,128)S(1)} %get-tuple-element.24), channel_id=1, source_target_pairs={{0,4},{4,8},{8,12},{1,5},{5,9},{9,13},{2,6},{6,10},{10,14},{3,7},{... | collective-permute-start | bytes 49160 | tf_op jit(solution)/shard_map/ppermute | solution.py:51
  127.2 0.0 copy-done.2
  127.2 0.0 copy-done.6
  127.2 1.3 add_add_fusion
  128.5 0.1 collective-permute-done.9
  128.6 0.0 collective-permute-done.10
  128.7 0.0 collective-permute-done.11
  128.7 0.0 collective-permute-done.6
  128.7 0.0 collective-permute-done.7
  128.7 0.0 copy-done.4
  128.7 2.8 %fusion.11 = f32[16,32,256]{2,1,0:T(8,128)} fusion(f32[16,32,256]{2,1,0:T(8,128)S(1)} %copy-done.2, f32[16,32,256]{2,1,0:T(8,128)S(1)} %copy-done.4, f32[16,32,1]{2,1,0:T(8,128)} %collective-permute-done.11, f32[18,1,256]{2,1,0:T(1,128)S(1)} %pad.14, f32[18,1,256]{2,1,0:T(1,128)S(1)} %pad.15, f32[1,32,256]{2,1,0:T(8,128)S(1)} %collective-permute-done.6, ...), kind=kLoop, calls=%fused_computation.25 | loop fusion | flops 7602176 | bytes 3514368 | tf_op jit(solution)/shard_map/sub | solution.py:93
  131.5 10.8 %all-to-all-done.1 = f32[16,1,7168]{2,1,0:T(1,128)S(1)} async-done(((f32[16,1,7168]{2,1,0:T(1,128)}), f32[16,1,7168]{2,1,0:T(1,128)S(1)}, u32[]{:S(2)}, u32[]{:S(2)}) %all-to-all-start.1) | async-done | bytes 458784 | tf_op jit(solution)/shard_map/all_to_all | solution.py:70
  142.3 0.9 reduce_sum.9
  (17 shorter events, 0.1 us)
Async XLA Ops:
  0.6 1.4 copy-start
  0.6 9.4 %copy-start.8 = (f32[7168]{0:T(1024)S(1)}, f32[7168]{0:T(1024)}, u32[]{:S(2)}) copy-start(f32[7168]{0:T(1024)} %param.15) | copy-start | bytes 86020
  2.0 24.4 %copy-start.9 = (s32[2048]{0:T(1024)S(1)}, s32[2048]{0:T(1024)}, u32[]{:S(2)}) copy-start(s32[2048]{0:T(1024)} %param.16) | copy-start | bytes 24580
  2.0 19.1 %collective-permute-start = (f32[2,1,32,256]{3,2,1,0:T(8,128)S(1)}, f32[2,1,32,256]{3,2,1,0:T(8,128)S(1)}, u32[]{:S(2)}, u32[]{:S(2)}) collective-permute-start(f32[2,1,32,256]{3,2,1,0:T(8,128)S(1)} %get-tuple-element.18), channel_id=1, source_target_pairs={{0,16},{16,32},{32,48},{48,64},{64,80},{80,96},{96,112},{112,128},... | collective-permute-start | bytes 196616 | tf_op jit(solution)/shard_map/ppermute | solution.py:21
  5.5 15.6 %collective-permute-start.1 = (f32[2,1,32,256]{3,2,1,0:T(8,128)S(1)}, f32[2,1,32,256]{3,2,1,0:T(8,128)S(1)}, u32[]{:S(2)}, u32[]{:S(2)}) collective-permute-start(f32[2,1,32,256]{3,2,1,0:T(8,128)S(1)} %get-tuple-element.19), channel_id=1, source_target_pairs={{16,0},{32,16},{48,32},{64,48},{80,64},{96,80},{112,96},{128,112},... | collective-permute-start | bytes 196616 | tf_op jit(solution)/shard_map/ppermute | solution.py:22
  11.0 32.7 %all-to-all-start = ((f32[16,1,7168]{2,1,0:T(1,128)}), f32[16,1,7168]{2,1,0:T(1,128)S(1)}, u32[]{:S(2)}, u32[]{:S(2)}) async-start(f32[16,1,7168]{2,1,0:T(1,128)} %broadcast_in_dim.19), calls=%async_computation | async-start | bytes 917504 | tf_op jit(solution)/shard_map/all_to_all | solution.py:29
  21.2 5.5 %collective-permute-start.2 = (f32[2,18,1,256]{3,2,1,0:T(1,128)S(1)}, f32[2,18,1,256]{3,2,1,0:T(1,128)S(1)}, u32[]{:S(2)}, u32[]{:S(2)}) collective-permute-start(f32[2,18,1,256]{3,2,1,0:T(1,128)S(1)} %get-tuple-element.16), channel_id=1, source_target_pairs={{0,4},{4,8},{8,12},{1,5},{5,9},{9,13},{2,6},{6,10},{10,14},{3,7},{... | collective-permute-start | bytes 110600 | tf_op jit(solution)/shard_map/ppermute | solution.py:21
  25.1 5.9 %collective-permute-start.3 = (f32[2,18,1,256]{3,2,1,0:T(1,128)S(1)}, f32[2,18,1,256]{3,2,1,0:T(1,128)S(1)}, u32[]{:S(2)}, u32[]{:S(2)}) collective-permute-start(f32[2,18,1,256]{3,2,1,0:T(1,128)S(1)} %get-tuple-element.17), channel_id=1, source_target_pairs={{4,0},{8,4},{12,8},{5,1},{9,5},{13,9},{6,2},{10,6},{14,10},{7,3},{... | collective-permute-start | bytes 110600 | tf_op jit(solution)/shard_map/ppermute | solution.py:22
  31.4 3.3 %copy-start.10 = (s32[2048]{0:T(1024)S(1)}, s32[2048]{0:T(1024)}, u32[]{:S(2)}) copy-start(s32[2048]{0:T(1024)} %param.17) | copy-start | bytes 24580
  31.7 4.2 %collective-permute-start.4 = (f32[2,18,34,1]{2,0,3,1:T(2,128)S(1)}, f32[2,18,34,1]{2,0,3,1:T(2,128)S(1)}, u32[]{:S(2)}, u32[]{:S(2)}) collective-permute-start(f32[2,18,34,1]{2,0,3,1:T(2,128)S(1)} %copy.43), channel_id=1, source_target_pairs={{0,1},{1,2},{2,3},{4,5},{5,6},{6,7},{8,9},{9,10},{10,11},{12,13},{... | collective-permute-start | bytes 14696 | tf_op jit(solution)/shard_map/ppermute | solution.py:21
  33.4 8.7 %collective-permute-start.5 = (f32[2,18,34,1]{2,0,3,1:T(2,128)S(1)}, f32[2,18,34,1]{2,0,3,1:T(2,128)S(1)}, u32[]{:S(2)}, u32[]{:S(2)}) collective-permute-start(f32[2,18,34,1]{2,0,3,1:T(2,128)S(1)} %copy.44), channel_id=1, source_target_pairs={{1,0},{2,1},{3,2},{5,4},{6,5},{7,6},{9,8},{10,9},{11,10},{13,12},{... | collective-permute-start | bytes 14696 | tf_op jit(solution)/shard_map/ppermute | solution.py:22
  43.7 11.8 %copy-start.7 = (f32[2048]{0:T(1024)S(1)}, f32[2048]{0:T(1024)}, u32[]{:S(2)}) copy-start(f32[2048]{0:T(1024)} %param.18) | copy-start | bytes 24580
  55.5 10.9 %copy-start.3 = (f32[16,32,256]{2,1,0:T(8,128)S(1)}, f32[16,32,256]{2,1,0:T(8,128)}, u32[]{:S(2)}) copy-start(f32[16,32,256]{2,1,0:T(8,128)} %param.13) | copy-start | bytes 1572868
  69.8 19.1 %copy-start.1 = (f32[16,32,256]{2,1,0:T(8,128)}, f32[16,32,256]{2,1,0:T(8,128)S(1)}, u32[]{:S(2)}) copy-start(f32[16,32,256]{2,1,0:T(8,128)S(1)} %get-tuple-element.7) | copy-start | bytes 1572868
  70.8 57.9 %collective-permute-start.10 = (f32[16,32,1]{2,1,0:T(8,128)}, f32[16,32,1]{2,1,0:T(8,128)}, u32[]{:S(2)}, u32[]{:S(2)}) collective-permute-start(f32[16,32,1]{2,1,0:T(8,128)} %get-tuple-element.20), channel_id=1, source_target_pairs={{1,0},{2,1},{3,2},{5,4},{6,5},{7,6},{9,8},{10,9},{11,10},{13,12},{... | collective-permute-start | bytes 6152 | tf_op jit(solution)/shard_map/ppermute | solution.py:52
  72.1 56.6 %collective-permute-start.11 = (f32[16,32,1]{2,1,0:T(8,128)}, f32[16,32,1]{2,1,0:T(8,128)}, u32[]{:S(2)}, u32[]{:S(2)}) collective-permute-start(f32[16,32,1]{2,1,0:T(8,128)} %get-tuple-element.21), channel_id=1, source_target_pairs={{0,1},{1,2},{2,3},{4,5},{5,6},{6,7},{8,9},{9,10},{10,11},{12,13},{... | collective-permute-start | bytes 6152 | tf_op jit(solution)/shard_map/ppermute | solution.py:51
  81.7 46.9 %collective-permute-start.6 = (f32[1,32,256]{2,1,0:T(8,128)S(1)}, f32[1,32,256]{2,1,0:T(8,128)S(1)}, u32[]{:S(2)}, u32[]{:S(2)}) collective-permute-start(f32[1,32,256]{2,1,0:T(8,128)S(1)} %get-tuple-element.23), channel_id=1, source_target_pairs={{16,0},{32,16},{48,32},{64,48},{80,64},{96,80},{112,96},{128,112},... | collective-permute-start | bytes 98312 | tf_op jit(solution)/shard_map/ppermute | solution.py:52
  85.0 43.7 %collective-permute-start.7 = (f32[1,32,256]{2,1,0:T(8,128)S(1)}, f32[1,32,256]{2,1,0:T(8,128)S(1)}, u32[]{:S(2)}, u32[]{:S(2)}) collective-permute-start(f32[1,32,256]{2,1,0:T(8,128)S(1)} %get-tuple-element.22), channel_id=1, source_target_pairs={{0,16},{16,32},{32,48},{48,64},{64,80},{80,96},{96,112},{112,128},... | collective-permute-start | bytes 98312 | tf_op jit(solution)/shard_map/ppermute | solution.py:51
  87.6 35.8 %collective-permute-start.8 = (f32[16,1,256]{2,1,0:T(1,128)S(1)}, f32[16,1,256]{2,1,0:T(1,128)S(1)}, u32[]{:S(2)}, u32[]{:S(2)}) collective-permute-start(f32[16,1,256]{2,1,0:T(1,128)S(1)} %get-tuple-element.25), channel_id=1, source_target_pairs={{4,0},{8,4},{12,8},{5,1},{9,5},{13,9},{6,2},{10,6},{14,10},{7,3},{... | collective-permute-start | bytes 49160 | tf_op jit(solution)/shard_map/ppermute | solution.py:52
  101.0 26.2 %copy-start.2 = (f32[16,32,256]{2,1,0:T(8,128)S(1)}, f32[16,32,256]{2,1,0:T(8,128)}, u32[]{:S(2)}) copy-start(f32[16,32,256]{2,1,0:T(8,128)} %copy-done.1) | copy-start | bytes 1572868
  101.0 26.2 %copy-start.6 = (f32[16,32,256]{2,1,0:T(8,128)S(1)}, f32[16,32,256]{2,1,0:T(8,128)}, u32[]{:S(2)}) copy-start(f32[16,32,256]{2,1,0:T(8,128)} %param.12) | copy-start | bytes 1572868
  113.3 15.4 %copy-start.4 = (f32[16,32,256]{2,1,0:T(8,128)S(1)}, f32[16,32,256]{2,1,0:T(8,128)}, u32[]{:S(2)}) copy-start(f32[16,32,256]{2,1,0:T(8,128)} %param.13) | copy-start | bytes 1572868
  113.3 15.4 %copy-start.5 = (f32[16,32,256]{2,1,0:T(8,128)S(1)}, f32[16,32,256]{2,1,0:T(8,128)}, u32[]{:S(2)}) copy-start(f32[16,32,256]{2,1,0:T(8,128)} %reshape.25) | copy-start | bytes 1572868
  113.3 29.0 %all-to-all-start.1 = ((f32[16,1,7168]{2,1,0:T(1,128)}), f32[16,1,7168]{2,1,0:T(1,128)S(1)}, u32[]{:S(2)}, u32[]{:S(2)}) async-start(f32[16,1,7168]{2,1,0:T(1,128)} %bitcast.6), calls=%async_computation.1 | async-start | bytes 917504 | tf_op jit(solution)/shard_map/all_to_all | solution.py:70
  123.4 5.3 %collective-permute-start.9 = (f32[16,1,256]{2,1,0:T(1,128)S(1)}, f32[16,1,256]{2,1,0:T(1,128)S(1)}, u32[]{:S(2)}, u32[]{:S(2)}) collective-permute-start(f32[16,1,256]{2,1,0:T(1,128)S(1)} %get-tuple-element.24), channel_id=1, source_target_pairs={{0,4},{4,8},{8,12},{1,5},{5,9},{9,13},{2,6},{6,10},{10,14},{3,7},{... | collective-permute-start | bytes 49160 | tf_op jit(solution)/shard_map/ppermute | solution.py:51
where the time goes:
time: 144 us; the launch traced here: 143 us
  starting transfers between devices  57.7 us (40%)
  local copies, waits for them, and re-layouts  38.6 us (27%)
  other arithmetic  24 us (17%)
  waiting for transfers between devices  21.2 us (15%)
  between operations  1.72 us (1%)
    ppermute x3, starting transfers between devices, extended(): lax.ppermute(last, axis, up)  16.1 us
    scatter-add x1, other arithmetic, on_device(): spread = jnp.zeros((coef_slab.shape[0],), jnp.float32).at[boundary_conduc...  12.3 us
    gather x1, local copies, waits for them, and re-layouts, on_device(): values = coef_slab[boundary_conductance_locator - slab_start]  11.8 us
    gather x1, local copies, waits for them, and re-layouts, on_device(): slot_grad = weight * heat_sink_gradient.reshape(-1)[boundary_voxel_locator]  11.8 us
    all_to_all x1, waiting for transfers between devices, summed_on_arrival(): lax.all_to_all(parts, axis, split_axis=0, concat_axis=0, tiled=True)  10.8 us
    all_to_all x1, starting transfers between devices, copy_for_each(): return lax.all_to_all(copies, axis, split_axis=0, concat_axis=0, tiled=True)  10.1 us
    all_to_all x1, starting transfers between devices, summed_on_arrival(): lax.all_to_all(parts, axis, split_axis=0, concat_axis=0, tiled=True)  10.1 us
    ppermute x3, waiting for transfers between devices, padded_2(): after = lax.ppermute(leading, axis, down)  9.97 us
  transfers between devices with their start and end apart: 14, of which 5 were waited for; matrix products, arithmetic and copies ran while one was open for 23% of the time, Pallas kernels for 0%

commit v1 on v0

v1 whole, which is shorter than its diff:
```python
import functools

import jax
import jax.numpy as jnp
from jax import lax
from jax.experimental import pallas as pl
from jax.experimental.pallas import tpu as pltpu
from jax.sharding import PartitionSpec as P

MESH = pl.DeviceIdType.MESH
F32 = jnp.float32
BF16 = jnp.bfloat16
I32 = jnp.int32

NX, NY, NZ = 16, 32, 256
ROWS = NX * NY
SLOTS = 2048
CHUNK = 7168
CROWS = CHUNK // 128
HROWS = 4 * CROWS
SLAB = 16 * CHUNK
STEP = 512

sharpness = 4.0
kinetic_fast = 0.6
kinetic_slow = 0.2
enthalpy = 0.4
bath = -2.0


def halves(x):
    high = x.astype(BF16)
    return high, (x - high.astype(F32)).astype(BF16)


def one_hot(index, column, size):
    column = jnp.concatenate([column] * (index.shape[1] // 128), axis=1)
    hit = column == jnp.broadcast_to(index, (size, index.shape[1]))
    return jnp.where(hit, jnp.ones((), BF16), jnp.zeros((), BF16))


def row_hit(index, size):
    rows = lax.broadcasted_iota(I32, (size, index.shape[1]), 0)
    return rows == index


def gate(t):
    return jax.nn.sigmoid(sharpness * (0.0 - t))


def rate(status):
    return jnp.where(status == 1, kinetic_fast, jnp.where(status == 2, kinetic_slow, 0.0))


def steps(count, body):
    @pl.loop(0, count)
    def _(k):
        body(pl.ds(pl.multiple_of(k * STEP, STEP), STEP))


def decode(loc, gx, zh):
    local = loc - gx * SLAB
    row = local >> 7
    owner = (row * 1171) >> 16
    inner = row - owner * CROWS
    mine = ((owner >> 1) & 1) == zh
    return jnp.where(mine, (owner >> 2) * CROWS + inner, -1), (owner & 1) * 128 + (local & 127)


def neighbours(center, low, high, y_low, y_high, z_edge):
    y = lax.broadcasted_iota(I32, (NY, NZ), 0)
    z = lax.broadcasted_iota(I32, (NY, NZ), 1)
    edge = jnp.concatenate([z_edge, z_edge], axis=1)
    total = low + high
    total = total + jnp.where(y == 0, y_low, pltpu.roll(center, 1, 0))
    total = total + jnp.where(y == NY - 1, y_high, pltpu.roll(center, NY - 1, 0))
    total = total + jnp.where(z == 0, edge, pltpu.roll(center, 1, 1))
    return total + jnp.where(z == NZ - 1, edge, pltpu.roll(center, NZ - 1, 1))


def z_faces(x):
    x = x.reshape(ROWS, NZ)
    lane = lax.broadcasted_iota(I32, (ROWS, 128), 1)
    both = jnp.where(lane == 0, x[:, :128], x[:, 128:]).T
    return both[0:1, :], both[127:128, :]


def z_block(left, right):
    row = lax.broadcasted_iota(I32, (128, ROWS), 0)
    both = jnp.where(row == 0, left, jnp.where(row == 127, right, 0.0))
    return both.T.reshape(NX, NY, 128)


def kernel(
    active,
    t0_hbm,
    f0_hbm,
    dn_hbm,
    st_hbm,
    coef_hbm,
    cell_hbm,
    loc_hbm,
    ext_hbm,
    te_hbm,
    pe_hbm,
    temp_out,
    frac_out,
    sens_out,
    t0p,
    wp,
    t1p,
    f0,
    dn,
    st,
    te,
    pe,
    tb,
    f1,
    bf,
    cf,
    t2,
    f2,
    tab,
    rs,
    spread,
    sens,
    cell,
    loc,
    ploc,
    ext,
    lane_c,
    row_c,
    lane_a,
    row_a,
    lane_b,
    row_b,
    val_a,
    val_b,
    ret,
    sg,
    psg,
    ys,
    yr,
    ys1,
    yr1,
    zs,
    zr,
    zs1,
    zr1,
    zt,
    gfield,
    sink,
    acc,
    tmat,
    gmat,
    oh_lane,
    column,
    load_sem,
    send_sem,
    recv_sem,
    out_sem,
):
    gx, gy, gz = lax.axis_index("gx"), lax.axis_index("gy"), lax.axis_index("gz")
    zh, c = gz // 2, gz % 2
    even = c == 0
    outer_live = jnp.logical_or(gz == 1, gz == 2)
    partner = (gx, gy, 3 - gz)
    mate = (gx, gy, zh * 2 + (1 - c))
    x_up, x_down = (lax.rem(gx + 1, 16), gy, gz), (lax.rem(gx + 15, 16), gy, gz)
    y_up, y_down = (gx, lax.rem(gy + 1, 4), gz), (gx, lax.rem(gy + 3, 4), gz)
    peers = []
    for j in range(1, 8):
        pgy, pc = lax.rem(gy + j // 2, 4), lax.rem(c + j % 2, 2)
        peers.append((j, pgy, pc, (gx, pgy, zh * 2 + pc)))

    barrier = pltpu.get_barrier_semaphore()
    met = [x_up, x_down, partner] + [p[3] for p in peers]
    for device in met:
        pl.semaphore_signal(barrier, inc=1, device_id=device, device_id_type=MESH)

    loads = {}
    for k, (name, source, target) in enumerate(
        (
            ("t0", t0_hbm, t0p.at[pl.ds(1, NX)]),
            ("dn", dn_hbm, dn),
            ("te", te_hbm, te),
            ("cell", cell_hbm, cell),
            ("loc", loc_hbm, loc),
            ("ext", ext_hbm, ext),
            ("coef", coef_hbm, tab.at[gy, c]),
            ("f0", f0_hbm, f0),
            ("st", st_hbm, st),
            ("pe", pe_hbm, pe),
        )
    ):
        loads[name] = pltpu.make_async_copy(source, target, load_sem.at[k])
        loads[name].start()

    sent = []

    def send(source, target, index, device):
        copy = pltpu.make_async_remote_copy(
            src_ref=source,
            dst_ref=target,
            send_sem=send_sem.at[index],
            recv_sem=recv_sem.at[index],
            device_id=device,
            device_id_type=MESH,
        )
        copy.start()
        sent.append(copy)
        return copy

    base = lax.broadcasted_iota(I32, (256, 128), 0).astype(F32).astype(BF16)
    column[...] = base

    loads["t0"].wait()
    loads["dn"].wait()
    loads["te"].wait()

    @pl.loop(0, NX)
    def _(i):
        wp[i + 1] = dn[i] * te[i]

    for k, padded in enumerate((t0p, wp)):
        ys[0, k] = padded[1:17, 0:1, :]
        ys[1, k] = padded[1:17, NY - 1 : NY, :]
        left, right = z_faces(padded[1:17])
        zs[0, k : k + 1] = jnp.where(even, right, left)
        zs[1, k : k + 1] = jnp.where(even, left, right)

    pl.semaphore_wait(barrier, len(met))

    to_partner = send(loc_hbm, ploc, 0, partner)
    table = [send(coef_hbm, tab.at[gy, c], j, device) for j, _, _, device in peers]
    halo = [
        send(zs.at[1], zr.at[1], 8, partner),
        send(zs.at[0], zr.at[0], 9, mate),
        send(t0p.at[1], t0p.at[NX + 1], 10, x_down),
        send(t0p.at[NX], t0p.at[0], 11, x_up),
        send(wp.at[1], wp.at[NX + 1], 12, x_down),
        send(wp.at[NX], wp.at[0], 13, x_up),
        send(ys.at[0], yr.at[1], 14, y_down),
        send(ys.at[1], yr.at[0], 15, y_up),
    ]

    for name in ("cell", "loc", "ext"):
        loads[name].wait()
    lane_c[...] = (cell[...] & (NZ - 1)).astype(F32)
    row_c[...] = cell[...] >> 8
    row, lane = decode(loc[...], gx, zh)
    row_a[...], lane_a[...] = row, lane.astype(F32)
    slot = lax.broadcasted_iota(I32, (1, SLOTS), 1)
    ext[...] = jnp.where(slot < active[0], ext[...], 0.0)

    def make_cells(cols):
        oh_lane[:, cols] = one_hot(lane_c[:, cols].astype(BF16), column[...], NZ)

    steps(SLOTS // STEP, make_cells)
    for name in ("f0", "st", "pe"):
        loads[name].wait()

    for copy in halo:
        copy.wait_recv()
    for padded in (t0p, wp):
        padded[0] = jnp.where(gx > 0, padded[0], 0.0)
        padded[NX + 1] = jnp.where(gx < 15, padded[NX + 1], 0.0)
    yr[0] = jnp.where(gy > 0, yr[0], 0.0)
    yr[1] = jnp.where(gy < 3, yr[1], 0.0)

    def z_halo(inner, outer):
        outer = jnp.where(outer_live, outer, 0.0)
        return z_block(jnp.where(even, outer, inner), jnp.where(even, inner, outer))

    for k in range(2):
        zt[k] = z_halo(zr[0, k : k + 1], zr[1, k : k + 1])

    @pl.loop(0, NX)
    def _(i):
        t = t0p[i + 1]
        around = neighbours(t, t0p[i], t0p[i + 2], yr[0, 0, i], yr[1, 0, i], zt[0, i])
        adjoint = neighbours(wp[i + 1], wp[i], wp[i + 2], yr[0, 1, i], yr[1, 1, i], zt[1, i])
        d, tw = dn[i], te[i]
        growth = rate(st[i]) * (1.0 - f0[i]) * gate(t)
        tb[i] = t + d * (around - 6.0 * t) + enthalpy * growth
        new = f0[i] + growth
        f1[i] = new
        bf[i] = tw * (1.0 - 6.0 * d) + adjoint
        cf[i] = (enthalpy * tw + pe[i]) * (rate(st[i]) * (1.0 - new)) * -sharpness

    def gather(matrix, size, lane_ref, row_ref, out, stored=None):
        def chunk(cols):
            if stored is None:
                hot = one_hot(lane_ref[:, cols].astype(BF16), column[...], 256)
            else:
                hot = stored[:, cols]
            found = jnp.dot(
                matrix[...],
                jnp.concatenate([hot, hot], axis=0),
                preferred_element_type=F32,
            )
            found = jnp.where(row_hit(row_ref[:, cols], size), found, 0.0)
            out[:, cols] = jnp.sum(found, axis=0, keepdims=True)

        steps(SLOTS // STEP, chunk)

    def scatter(value, size, lane_ref, row_ref, out, stored=None):
        def chunk(cols):
            if stored is None:
                hot = one_hot(lane_ref[:, cols].astype(BF16), column[...], 256)
            else:
                hot = stored[:, cols]
            high, low = halves(value[:, cols])
            right = jnp.concatenate(
                [hot * jnp.broadcast_to(high, hot.shape), hot * jnp.broadcast_to(low, hot.shape)],
                axis=1,
            )
            left = jnp.where(row_hit(row_ref[:, cols], size), 1.0, 0.0).astype(BF16)
            out[...] += lax.dot_general(
                jnp.concatenate([left, left], axis=1),
                right,
                (((1,), (1,)), ((), ())),
                preferred_element_type=F32,
            )

        steps(SLOTS // STEP, chunk)

    loads["coef"].wait()
    to_partner.wait_recv()
    for copy in table:
        copy.wait_recv()
    row, lane = decode(ploc[...], gx, zh)
    row_b[...], lane_b[...] = row, lane.astype(F32)
    pieces = []
    for part in range(2):
        pieces.append(halves(tab[:, part].reshape(HROWS, 128)))
    tmat[...] = jnp.concatenate(
        [pieces[0][0], pieces[1][0], pieces[0][1], pieces[1][1]], axis=1
    )
    gather(tmat, HROWS, lane_b, row_b, val_b)
    reply = send(val_b, ret, 16, partner)
    gather(tmat, HROWS, lane_a, row_a, val_a)
    reply.wait_recv()
    val_a[...] = ext[...] * (val_a[...] + ret[...])
    sink[...] = jnp.zeros_like(sink)
    scatter(val_a, ROWS, lane_c, row_c, sink, oh_lane)

    @pl.loop(0, NX)
    def _(i):
        rows = pl.ds(pl.multiple_of(i * NY, NY), NY)
        t, drain, tw, d = t0p[i + 1], sink[rows, :], te[i], dn[i]
        lifted = t - bath
        t1 = tb[i] - drain * lifted
        t1p[i + 1] = t1
        g = gate(t1)
        growth = rate(st[i]) * (1.0 - f1[i]) * g
        f2[i] = f1[i] + growth
        t2[i] = t1 - 6.0 * d * t1 + enthalpy * growth - drain * (t1 - bath)
        dual = bf[i] - tw * drain + cf[i] * g * (1.0 - g)
        high, low = halves(-(tw * (t1 - bath) + dual * lifted))
        gmat[rows, 0:NZ] = high
        gmat[rows, NZ : 2 * NZ] = low

    frac_copy = pltpu.make_async_copy(f2, frac_out, out_sem.at[0])
    frac_copy.start()
    gather(gmat, ROWS, lane_c, row_c, sg, oh_lane)
    sg[...] = ext[...] * sg[...]
    slots = send(sg, psg, 17, partner)

    ys1[0] = t1p[1:17, 0:1, :]
    ys1[1] = t1p[1:17, NY - 1 : NY, :]
    left, right = z_faces(t1p[1:17])
    zs1[0] = jnp.where(even, right, left)
    zs1[1] = jnp.where(even, left, right)
    halo = [
        send(zs1.at[1], zr1.at[1], 18, partner),
        send(zs1.at[0], zr1.at[0], 19, mate),
        send(t1p.at[1], t1p.at[NX + 1], 20, x_down),
        send(t1p.at[NX], t1p.at[0], 21, x_up),
        send(ys1.at[0], yr1.at[1], 22, y_down),
        send(ys1.at[1], yr1.at[0], 23, y_up),
    ]
    acc[...] = jnp.zeros_like(acc)
    scatter(sg, HROWS, lane_a, row_a, acc)
    slots.wait_recv()
    scatter(psg, HROWS, lane_b, row_b, acc)
    for g in range(4):
        for part in range(2):
            spread[g, part] = acc[g * CROWS : (g + 1) * CROWS, part * 128 : (part + 1) * 128]
    shares = [
        send(spread.at[pgy, pc], rs.at[j], 23 + j, device) for j, pgy, pc, device in peers
    ]

    for copy in halo:
        copy.wait_recv()
    t1p[0] = jnp.where(gx > 0, t1p[0], 0.0)
    t1p[NX + 1] = jnp.where(gx < 15, t1p[NX + 1], 0.0)
    yr1[0] = jnp.where(gy > 0, yr1[0], 0.0)
    yr1[1] = jnp.where(gy < 3, yr1[1], 0.0)
    zt[0] = z_halo(zr1[0], zr1[1])

    @pl.loop(0, NX)
    def _(i):
        around = neighbours(
            t1p[i + 1], t1p[i], t1p[i + 2], yr1[0, i], yr1[1, i], zt[0, i]
        )
        t2[i] = t2[i] + dn[i] * around

    temp_copy = pltpu.make_async_copy(t2, temp_out, out_sem.at[1])
    temp_copy.start()
    total = spread[gy, c]
    for copy, (j, _, _, _) in zip(shares, peers):
        copy.wait_recv()
        total = total + rs[j]
    sens[...] = total
    sens_copy = pltpu.make_async_copy(sens, sens_out, out_sem.at[2])
    sens_copy.start()
    for copy in sent:
        copy.wait_send()
    frac_copy.wait()
    temp_copy.wait()
    sens_copy.wait()


def on_device(t0, f0, dn, st, coef, cell, loc, ext, active, te, pe):
    field = (NX, NY, NZ)
    padded = (NX + 2, NY, NZ)
    row = (1, SLOTS)
    vmem = pltpu.VMEM
    anywhere = pl.BlockSpec(memory_space=pl.ANY)
    scratch = (
        [vmem(padded, F32)] * 3
        + [vmem(field, F32)] * 2
        + [vmem(field, I32)]
        + [vmem(field, F32)] * 8
        + [
            vmem((4, 2, CROWS, 128), F32),
            vmem((8, CROWS, 128), F32),
            vmem((4, 2, CROWS, 128), F32),
            vmem((CROWS, 128), F32),
            vmem(row, I32),
            vmem(row, I32),
            vmem(row, I32),
            vmem(row, F32),
        ]
        + [vmem(row, F32), vmem(row, I32)] * 3
        + [vmem(row, F32)] * 5
        + [vmem((2, 2, NX, 1, NZ), F32)] * 2
        + [vmem((2, NX, 1, NZ), F32)] * 2
        + [vmem((2, 2, ROWS), F32)] * 2
        + [vmem((2, 1, ROWS), F32)] * 2
        + [
            vmem((2, NX, NY, 128), F32),
            vmem((8, 128), F32),
            vmem((ROWS, NZ), F32),
            vmem((HROWS, 256), F32),
            vmem((HROWS, 512), BF16),
            vmem((ROWS, 512), BF16),
            vmem((NZ, SLOTS), BF16),
            vmem((256, 128), BF16),
            pltpu.SemaphoreType.DMA((10,)),
            pltpu.SemaphoreType.DMA((31,)),
            pltpu.SemaphoreType.DMA((31,)),
            pltpu.SemaphoreType.DMA((3,)),
        ]
    )
    temp, frac, sens = pl.pallas_call(
        kernel,
        out_shape=(
            jax.ShapeDtypeStruct(field, F32),
            jax.ShapeDtypeStruct(field, F32),
            jax.ShapeDtypeStruct((CROWS, 128), F32),
        ),
        in_specs=[pl.BlockSpec(memory_space=pltpu.SMEM)] + [anywhere] * 10,
        out_specs=(anywhere,) * 3,
        scratch_shapes=scratch,
        compiler_params=pltpu.CompilerParams(
            collective_id=0, has_side_effects=True, vmem_limit_bytes=56 * 2**20
        ),
    )(
        active,
        t0,
        f0,
        dn,
        st,
        coef.reshape(CROWS, 128),
        cell.reshape(row),
        loc.reshape(row),
        ext.reshape(row),
        te,
        pe,
    )
    return temp, frac, sens.reshape(CHUNK)


def solution(mesh):
    brick, line = P("gx", "gy", "gz"), P(("gx", "gy", "gz"))
    return jax.shard_map(
        on_device,
        mesh=mesh,
        in_specs=(brick,) * 4 + (line,) * 5 + (brick,) * 2,
        out_specs=(brick, brick, line),
        check_vma=False,
    )
```

time: 144 us -> 45.7 us (0.32)
  the two profiles are of different devices: /device:TPU:32 before, /device:TPU:1 now
where the time goes in v1:
time: 45.7 us; the launch traced here: 45.6 us
  Pallas kernels  40.9 us (89%)
  local copies, waits for them, and re-layouts  3.35 us (7%)
  between operations  1.3 us (3%)
    pallas_call x1, Pallas kernels, on_device(): pl.pallas_call(kernel, out_shape=(jax.ShapeDtypeStruct(field, F32), jax.S...  40.9 us
    unnamed x7, local copies, waits for them, and re-layouts  3.35 us

profile of v1, /device:TPU:1, one launch (start us, length us, event | category | flops | bytes accessed | tf_op | source)
XLA Modules:
  0.0 45.6 jit_solution(16644529486404771433)
XLA Ops:
  1.3 40.9 %shard_map.130 = (f32[16,32,256]{2,1,0:T(8,128)}, f32[16,32,256]{2,1,0:T(8,128)}, f32[56,128]{1,0:T(8,128)}) custom-call(s32[1]{0:T(128)S(6)} %copy.17.active, f32[16,32,256]{2,1,0:T(8,128)} %t0_hbm.1, f32[16,32,256]{2,1,0:T(8,128)} %f0_hbm.1, f32[16,32,256]{2,1,0:T(8,128)} %dn_hbm.1, s32[16,32,256]{2,1,0:T(8,128)} %st_hbm.1, f32[56,128]{1,0:T(8,128)} %bitcast.5, ...), custom_call_target="tpu_custom_call" | custom-call | tf_op jit(solution)/shard_map/pallas_call | solution.py:467
  42.2 0.0 copy-start
  42.2 1.9 %copy.18 = f32[16,32,256]{2,1,0:T(8,128)} copy(f32[16,32,256]{2,1,0:T(8,128)} %get-tuple-element.12) | data formatting | bytes 1048576
  44.1 0.0 copy-done
  44.2 0.0 copy-start.1
  44.2 0.8 %copy.19 = f32[16,32,256]{2,1,0:T(8,128)} copy(f32[16,32,256]{2,1,0:T(8,128)S(1)} %copy-done) | data formatting | bytes 1048576
  44.9 0.0 copy-done.1
  44.9 0.6 %copy.20 = f32[7168]{0:T(1024)} copy(f32[7168]{0:T(1024)S(1)} %bitcast.6) | data formatting | bytes 57344
Async XLA Ops:
  42.2 2.0 %copy-start = (f32[16,32,256]{2,1,0:T(8,128)S(1)}, f32[16,32,256]{2,1,0:T(8,128)}, u32[]{:S(2)}) copy-start(f32[16,32,256]{2,1,0:T(8,128)} %get-tuple-element.13) | copy-start | bytes 1572868
  44.2 0.8 %copy-start.1 = (f32[56,128]{1,0:T(8,128)S(1)}, f32[56,128]{1,0:T(8,128)}, u32[]{:S(2)}) copy-start(f32[56,128]{1,0:T(8,128)} %get-tuple-element.8) | copy-start | bytes 86020

commit v2 on v1

v2 whole, which is shorter than its diff:
```python
import functools

import jax
import jax.numpy as jnp
from jax import lax
from jax.experimental import pallas as pl
from jax.experimental.pallas import tpu as pltpu
from jax.sharding import PartitionSpec as P

MESH = pl.DeviceIdType.MESH
F32 = jnp.float32
BF16 = jnp.bfloat16
I32 = jnp.int32

NX, NY, NZ = 16, 32, 256
ROWS = NX * NY
SLOTS = 2048
CHUNK = 7168
CROWS = CHUNK // 128
HROWS = 4 * CROWS
SLAB = 16 * CHUNK

sharpness = 4.0
kinetic_fast = 0.6
kinetic_slow = 0.2
enthalpy = 0.4
bath = -2.0


def halves(x):
    high = x.astype(BF16)
    return high, (x - high.astype(F32)).astype(BF16)


def one_hot(index, column, size):
    column = jnp.concatenate([column] * (index.shape[1] // 128), axis=1)
    hit = column == jnp.broadcast_to(index, (size, index.shape[1]))
    return jnp.where(hit, jnp.ones((), BF16), jnp.zeros((), BF16))


def row_hit(index, size):
    rows = lax.broadcasted_iota(I32, (size, index.shape[1]), 0)
    return rows == index


def gate(t):
    return jax.nn.sigmoid(sharpness * (0.0 - t))


def rate(status):
    return jnp.where(status == 1, kinetic_fast, jnp.where(status == 2, kinetic_slow, 0.0))


def decode(loc, gx, zh):
    local = loc - gx * SLAB
    row = local >> 7
    owner = (row * 1171) >> 16
    inner = row - owner * CROWS
    mine = ((owner >> 1) & 1) == zh
    return jnp.where(mine, (owner >> 2) * CROWS + inner, -1), (owner & 1) * 128 + (local & 127)


def neighbours(center, low, high, y_low, y_high, z_edge):
    y = lax.broadcasted_iota(I32, (NY, NZ), 0)
    z = lax.broadcasted_iota(I32, (NY, NZ), 1)
    edge = jnp.concatenate([z_edge, z_edge], axis=1)
    total = low + high
    total = total + jnp.where(y == 0, y_low, pltpu.roll(center, 1, 0))
    total = total + jnp.where(y == NY - 1, y_high, pltpu.roll(center, NY - 1, 0))
    total = total + jnp.where(z == 0, edge, pltpu.roll(center, 1, 1))
    return total + jnp.where(z == NZ - 1, edge, pltpu.roll(center, NZ - 1, 1))


def z_faces(x):
    x = x.reshape(ROWS, NZ)
    lane = lax.broadcasted_iota(I32, (ROWS, 128), 1)
    both = jnp.where(lane == 0, x[:, :128], x[:, 128:]).T
    return both[0:1, :], both[127:128, :]


def z_block(left, right):
    row = lax.broadcasted_iota(I32, (128, ROWS), 0)
    both = jnp.where(row == 0, left, jnp.where(row == 127, right, 0.0))
    return both.T.reshape(NX, NY, 128)


def kernel(
    active,
    t0_hbm,
    f0_hbm,
    dn_hbm,
    st_hbm,
    coef_hbm,
    cell_hbm,
    loc_hbm,
    ext_hbm,
    te_hbm,
    pe_hbm,
    t2,
    f2,
    sens,
    t0p,
    wp,
    t1p,
    f0,
    dn,
    st,
    te,
    pe,
    tb,
    f1,
    tab,
    rs,
    spread,
    cell,
    loc,
    ploc,
    ext,
    row_c,
    lane_a,
    row_a,
    lane_b,
    row_b,
    val_a,
    val_b,
    ret,
    sg,
    psg,
    ys,
    yr,
    ys1,
    yr1,
    zs,
    zr,
    zs1,
    zr1,
    zt,
    sink,
    acc,
    tmat,
    fmat,
    fv,
    oh_lane,
    column,
    load_sem,
    send_sem,
    recv_sem,
):
    gx, gy, gz = lax.axis_index("gx"), lax.axis_index("gy"), lax.axis_index("gz")
    zh, c = gz // 2, gz % 2
    even = c == 0
    outer_live = jnp.logical_or(gz == 1, gz == 2)
    partner = (gx, gy, 3 - gz)
    mate = (gx, gy, zh * 2 + (1 - c))
    x_up, x_down = (jnp.minimum(gx + 1, 15), gy, gz), (jnp.maximum(gx - 1, 0), gy, gz)
    has_up, has_down = gx < 15, gx > 0
    first, second = zh == 0, zh == 1
    y_up, y_down = (gx, lax.rem(gy + 1, 4), gz), (gx, lax.rem(gy + 3, 4), gz)
    peers = []
    for j in range(1, 8):
        pgy, pc = lax.rem(gy + j // 2, 4), lax.rem(c + j % 2, 2)
        peers.append((j, pgy, pc, (gx, pgy, zh * 2 + pc)))

    barrier = pltpu.get_barrier_semaphore()

    def greet(device):
        pl.semaphore_signal(barrier, inc=1, device_id=device, device_id_type=MESH)

    pl.when(first)(lambda: greet(partner))
    pl.when(has_up)(lambda: greet(x_up))
    pl.when(has_down)(lambda: greet(x_down))
    for _, _, _, device in peers:
        greet(device)
    expected = 7 + has_up.astype(I32) + has_down.astype(I32) + zh

    loads = {}
    for k, (name, source, target) in enumerate(
        (
            ("t0", t0_hbm, t0p.at[pl.ds(1, NX)]),
            ("dn", dn_hbm, dn),
            ("te", te_hbm, te),
            ("cell", cell_hbm, cell),
            ("loc", loc_hbm, loc),
            ("ext", ext_hbm, ext),
            ("coef", coef_hbm, tab.at[gy, c]),
            ("f0", f0_hbm, f0),
            ("st", st_hbm, st),
            ("pe", pe_hbm, pe),
        )
    ):
        loads[name] = pltpu.make_async_copy(source, target, load_sem.at[k])
        loads[name].start()

    sent = []

    def remote(source, target, index, device):
        return pltpu.make_async_remote_copy(
            src_ref=source,
            dst_ref=target,
            send_sem=send_sem.at[index],
            recv_sem=recv_sem.at[index],
            device_id=device,
            device_id_type=MESH,
        )

    def send(source, target, index, device):
        copy = remote(source, target, index, device)
        copy.start()
        sent.append(copy.wait_send)
        return copy

    def send_x(padded, index):
        down = remote(padded.at[1], padded.at[NX + 1], index, x_down)
        up = remote(padded.at[NX], padded.at[0], index + 1, x_up)
        pl.when(has_down)(down.start)
        pl.when(has_up)(up.start)
        sent.append(lambda: pl.when(has_down)(down.wait_send))
        sent.append(lambda: pl.when(has_up)(up.wait_send))

        def arrived():
            pl.when(has_up)(down.wait_recv)
            pl.when(has_down)(up.wait_recv)
            padded[0] = jnp.where(has_down, padded[0], 0.0)
            padded[NX + 1] = jnp.where(has_up, padded[NX + 1], 0.0)

        return arrived

    base = lax.broadcasted_iota(I32, (256, 128), 0).astype(F32).astype(BF16)
    column[...] = base

    loads["t0"].wait()
    loads["dn"].wait()
    loads["te"].wait()

    @pl.loop(0, NX)
    def _(i):
        wp[i + 1] = dn[i] * te[i]

    for k, padded in enumerate((t0p, wp)):
        ys[0, k] = padded[1:17, 0:1, :]
        ys[1, k] = padded[1:17, NY - 1 : NY, :]
        left, right = z_faces(padded[1:17])
        zs[0, k : k + 1] = jnp.where(even, right, left)
        zs[1, k : k + 1] = jnp.where(even, left, right)

    pl.semaphore_wait(barrier, expected)
    table = [send(coef_hbm, tab.at[gy, c], j, device) for j, _, _, device in peers]
    request = remote(loc_hbm, ploc, 0, partner)
    outer = remote(zs.at[1], zr.at[1], 8, partner)

    def ask():
        request.start()
        outer.start()

    pl.when(second)(ask)
    halo = [
        send(zs.at[0], zr.at[0], 9, mate),
        send(ys.at[0], yr.at[1], 14, y_down),
        send(ys.at[1], yr.at[0], 15, y_up),
    ]
    halo_x = [send_x(t0p, 10), send_x(wp, 12)]
    sent.append(request.wait_send)
    sent.append(outer.wait_send)

    for name in ("cell", "loc", "ext"):
        loads[name].wait()
    cell_row = cell[...] >> 8
    oh_lane[...] = one_hot((cell[...] & (NZ - 1)).astype(F32).astype(BF16), column[...], NZ)
    row_c[...] = cell_row
    row, lane = decode(loc[...], gx, zh)
    row_a[...], lane_a[...] = row, lane.astype(F32)
    slot = lax.broadcasted_iota(I32, (1, SLOTS), 1)
    ext[...] = jnp.where(slot < active[0], ext[...], 0.0)
    for name in ("f0", "st", "pe"):
        loads[name].wait()

    def put(k, rows, x):
        high, low = halves(x)
        fmat[k, rows, 0:NZ] = high
        fmat[k, rows, NZ : 2 * NZ] = low

    @pl.loop(0, NX)
    def _(i):
        rows = pl.ds(pl.multiple_of(i * NY, NY), NY)
        t, tw = t0p[i + 1], te[i]
        lifted = t - bath
        growth = rate(st[i]) * (1.0 - f0[i]) * gate(t)
        new = f0[i] + growth
        f1[i] = new
        tb[i] = enthalpy * growth
        slope = (enthalpy * tw + pe[i]) * (rate(st[i]) * (1.0 - new)) * -sharpness
        put(0, rows, lifted)
        put(1, rows, tw * lifted)
        put(2, rows, slope * lifted)

    def gather(matrix, size, hot, row, out):
        found = jnp.dot(
            matrix[...], jnp.concatenate([hot, hot], axis=0), preferred_element_type=F32
        )
        found = jnp.where(row_hit(row, size), found, 0.0)
        out[...] = jnp.sum(found, axis=0, keepdims=True)

    def scatter(value, size, hot, row):
        high, low = halves(value)
        right = jnp.concatenate(
            [hot * jnp.broadcast_to(high, hot.shape), hot * jnp.broadcast_to(low, hot.shape)],
            axis=1,
        )
        left = jnp.where(row_hit(row, size), 1.0, 0.0).astype(BF16)
        return lax.dot_general(
            jnp.concatenate([left, left], axis=1),
            right,
            (((1,), (1,)), ((), ())),
            preferred_element_type=F32,
        )

    def hot_lanes(ref):
        return one_hot(ref[...].astype(BF16), column[...], 256)

    for k in range(3):
        gather(fmat.at[k], ROWS, oh_lane[...], row_c[...], fv.at[k])

    loads["coef"].wait()
    for copy in table:
        copy.wait_recv()
    pieces = []
    for part in range(2):
        pieces.append(halves(tab[:, part].reshape(HROWS, 128)))
    tmat[...] = jnp.concatenate(
        [pieces[0][0], pieces[1][0], pieces[0][1], pieces[1][1]], axis=1
    )
    gather(tmat, HROWS, hot_lanes(lane_a), row_a[...], val_a)

    request.wait_recv()
    pl.when(first)(ask)
    row, lane = decode(ploc[...], gx, zh)
    row_b[...], lane_b[...] = row, lane.astype(F32)
    gather(tmat, HROWS, hot_lanes(lane_b), row_b[...], val_b)
    reply = send(val_b, ret, 16, partner)

    for copy in halo:
        copy.wait_recv()
    for arrived in halo_x:
        arrived()
    outer.wait_recv()
    yr[0] = jnp.where(gy > 0, yr[0], 0.0)
    yr[1] = jnp.where(gy < 3, yr[1], 0.0)

    def z_halo(inner, outer):
        outer = jnp.where(outer_live, outer, 0.0)
        return z_block(jnp.where(even, outer, inner), jnp.where(even, inner, outer))

    for k in range(2):
        zt[k] = z_halo(zr[0, k : k + 1], zr[1, k : k + 1])

    @pl.loop(0, NX)
    def _(i):
        t = t0p[i + 1]
        around = neighbours(t, t0p[i], t0p[i + 2], yr[0, 0, i], yr[1, 0, i], zt[0, i])
        adjoint = neighbours(wp[i + 1], wp[i], wp[i + 2], yr[0, 1, i], yr[1, 1, i], zt[1, i])
        d, tw = dn[i], te[i]
        rows = pl.ds(pl.multiple_of(i * NY, NY), NY)
        plain = t + d * (around - 6.0 * t) + tb[i]
        tb[i] = plain
        put(3, rows, plain)
        put(4, rows, tw * (plain - bath) + (tw * (1.0 - 6.0 * d) + adjoint) * (t - bath))

    for k in range(3, 5):
        gather(fmat.at[k], ROWS, oh_lane[...], row_c[...], fv.at[k])

    reply.wait_recv()
    drain = ext[...] * (val_a[...] + ret[...])
    val_a[...] = drain
    g = gate(fv[3] - drain * fv[0])
    sg[...] = -ext[...] * (fv[4] - 2.0 * drain * fv[1] + fv[2] * (g * (1.0 - g)))
    slots = send(sg, psg, 17, partner)
    sink[...] = scatter(val_a[...], ROWS, oh_lane[...], row_c[...])

    @pl.loop(0, NX)
    def _(i):
        rows = pl.ds(pl.multiple_of(i * NY, NY), NY)
        drain = sink[rows, :]
        t1 = tb[i] - drain * (t0p[i + 1] - bath)
        t1p[i + 1] = t1
        growth = rate(st[i]) * (1.0 - f1[i]) * gate(t1)
        f2[i] = f1[i] + growth
        t2[i] = t1 - 6.0 * dn[i] * t1 + enthalpy * growth - drain * (t1 - bath)

    ys1[0] = t1p[1:17, 0:1, :]
    ys1[1] = t1p[1:17, NY - 1 : NY, :]
    left, right = z_faces(t1p[1:17])
    zs1[0] = jnp.where(even, right, left)
    zs1[1] = jnp.where(even, left, right)
    halo = [
        send(zs1.at[1], zr1.at[1], 18, partner),
        send(zs1.at[0], zr1.at[0], 19, mate),
        send(ys1.at[0], yr1.at[1], 22, y_down),
        send(ys1.at[1], yr1.at[0], 23, y_up),
    ]
    halo_x = send_x(t1p, 20)
    acc[...] = scatter(sg[...], HROWS, hot_lanes(lane_a), row_a[...])
    slots.wait_recv()
    acc[...] += scatter(psg[...], HROWS, hot_lanes(lane_b), row_b[...])
    for g in range(4):
        for part in range(2):
            spread[g, part] = acc[g * CROWS : (g + 1) * CROWS, part * 128 : (part + 1) * 128]
    shares = [
        send(spread.at[pgy, pc], rs.at[j], 23 + j, device) for j, pgy, pc, device in peers
    ]

    for copy in halo:
        copy.wait_recv()
    halo_x()
    yr1[0] = jnp.where(gy > 0, yr1[0], 0.0)
    yr1[1] = jnp.where(gy < 3, yr1[1], 0.0)
    zt[0] = z_halo(zr1[0], zr1[1])

    @pl.loop(0, NX)
    def _(i):
        around = neighbours(
            t1p[i + 1], t1p[i], t1p[i + 2], yr1[0, i], yr1[1, i], zt[0, i]
        )
        t2[i] = t2[i] + dn[i] * around

    total = spread[gy, c]
    for copy, (j, _, _, _) in zip(shares, peers):
        copy.wait_recv()
        total = total + rs[j]
    sens[...] = total
    for wait in sent:
        wait()


def deliver(t2, f2, sens, temp_out, frac_out, sens_out, sem):
    copies = [
        pltpu.make_async_copy(source, target, sem.at[k])
        for k, (source, target) in enumerate(((t2, temp_out), (f2, frac_out), (sens, sens_out)))
    ]
    for copy in copies:
        copy.start()
    for copy in copies:
        copy.wait()


def on_device(t0, f0, dn, st, coef, cell, loc, ext, active, te, pe):
    field = (NX, NY, NZ)
    padded = (NX + 2, NY, NZ)
    row = (1, SLOTS)
    vmem = pltpu.VMEM
    anywhere = pl.BlockSpec(memory_space=pl.ANY)
    scratch = (
        [vmem(padded, F32)] * 3
        + [vmem(field, F32)] * 2
        + [vmem(field, I32)]
        + [vmem(field, F32)] * 4
        + [
            vmem((4, 2, CROWS, 128), F32),
            vmem((8, CROWS, 128), F32),
            vmem((4, 2, CROWS, 128), F32),
            vmem(row, I32),
            vmem(row, I32),
            vmem(row, I32),
            vmem(row, F32),
        ]
        + [vmem(row, I32)]
        + [vmem(row, F32), vmem(row, I32)] * 2
        + [vmem(row, F32)] * 5
        + [vmem((2, 2, NX, 1, NZ), F32)] * 2
        + [vmem((2, NX, 1, NZ), F32)] * 2
        + [vmem((2, 2, ROWS), F32)] * 2
        + [vmem((2, 1, ROWS), F32)] * 2
        + [
            vmem((2, NX, NY, 128), F32),
            vmem((ROWS, NZ), F32),
            vmem((HROWS, 256), F32),
            vmem((HROWS, 512), BF16),
            vmem((5, ROWS, 512), BF16),
            vmem((5, 1, SLOTS), F32),
            vmem((NZ, SLOTS), BF16),
            vmem((256, 128), BF16),
            pltpu.SemaphoreType.DMA((10,)),
            pltpu.SemaphoreType.DMA((31,)),
            pltpu.SemaphoreType.DMA((31,)),
        ]
    )
    results = (
        jax.ShapeDtypeStruct(field, F32),
        jax.ShapeDtypeStruct(field, F32),
        jax.ShapeDtypeStruct((CROWS, 128), F32),
    )
    done = pl.pallas_call(
        kernel,
        out_shape=results,
        in_specs=[pl.BlockSpec(memory_space=pltpu.SMEM)] + [anywhere] * 10,
        out_specs=(pl.BlockSpec(memory_space=vmem),) * 3,
        scratch_shapes=scratch,
        compiler_params=pltpu.CompilerParams(
            collective_id=0, has_side_effects=True, vmem_limit_bytes=56 * 2**20
        ),
    )(
        active,
        t0,
        f0,
        dn,
        st,
        coef.reshape(CROWS, 128),
        cell.reshape(row),
        loc.reshape(row),
        ext.reshape(row),
        te,
        pe,
    )
    temp, frac, sens = pl.pallas_call(
        deliver,
        out_shape=results,
        in_specs=[pl.BlockSpec(memory_space=vmem)] * 3,
        out_specs=(anywhere,) * 3,
        scratch_shapes=[pltpu.SemaphoreType.DMA((3,))],
    )(*done)
    return temp, frac, sens.reshape(CHUNK)


def solution(mesh):
    brick, line = P("gx", "gy", "gz"), P(("gx", "gy", "gz"))
    return jax.shard_map(
        on_device,
        mesh=mesh,
        in_specs=(brick,) * 4 + (line,) * 5 + (brick,) * 2,
        out_specs=(brick, brick, line),
        check_vma=False,
    )
```

time: 45.7 us -> 38.3 us (0.84)
  Pallas kernels: 40.9 us -> 36.9 us
  local copies, waits for them, and re-layouts: 3.35 us -> 0 us
    pallas_call x1 -> x2, Pallas kernels: 40.9 us -> 36.9 us  [the longest x1 34.7 us: on_device(): pl.pallas_call(kernel, out_shape=results, in_specs=[pl.BlockSpec(memory_s...]
    unnamed x7 -> x0, local copies, waits for them, and re-layouts: 3.35 us -> none
where the time goes in v2:
time: 38.3 us; the launch traced here: 38.2 us
  Pallas kernels  36.9 us (96%)
  between operations  1.29 us (3%)
    pallas_call x1, Pallas kernels, on_device(): pl.pallas_call(kernel, out_shape=results, in_specs=[pl.BlockSpec(memory_s...  34.7 us
    pallas_call x1, Pallas kernels, on_device(): pl.pallas_call(deliver, out_shape=results, in_specs=[pl.BlockSpec(memory_...  2.2 us

profile of v2, /device:TPU:1, one launch (start us, length us, event | category | flops | bytes accessed | tf_op | source)
XLA Modules:
  0.0 38.2 jit_solution(11355152962661667973)
XLA Ops:
  1.3 34.7 %shard_map.130 = (f32[16,32,256]{2,1,0:T(8,128)}, f32[16,32,256]{2,1,0:T(8,128)}, f32[56,128]{1,0:T(8,128)}) custom-call(s32[1]{0:T(128)S(6)} %copy.14.active, f32[16,32,256]{2,1,0:T(8,128)} %t0_hbm.1, f32[16,32,256]{2,1,0:T(8,128)} %f0_hbm.1, f32[16,32,256]{2,1,0:T(8,128)} %dn_hbm.1, s32[16,32,256]{2,1,0:T(8,128)} %st_hbm.1, f32[56,128]{1,0:T(8,128)} %bitcast.5, ...), custom_call_target="tpu_custom_call" | custom-call | tf_op jit(solution)/shard_map/pallas_call | solution.py:491
  36.0 2.2 %shard_map.131 = (f32[16,32,256]{2,1,0:T(8,128)}, f32[16,32,256]{2,1,0:T(8,128)}, f32[56,128]{1,0:T(8,128)}) custom-call(f32[16,32,256]{2,1,0:T(8,128)} %get-tuple-element.9.t2, f32[16,32,256]{2,1,0:T(8,128)} %get-tuple-element.10.f2, f32[56,128]{1,0:T(8,128)} %get-tuple-element.11.sens), custom_call_target="tpu_custom_call" | custom-call | tf_op jit(solution)/shard_map/pallas_call | solution.py:513

commit v3 on v2

--- a/solution.py
+++ b/solution.py
@@ -19,6 +19,11 @@
 CROWS = CHUNK // 128
 HROWS = 4 * CROWS
 SLAB = 16 * CHUNK
+GROUP = 256
+GROUPS = SLOTS // GROUP
+WIDTH = 64
+WINDOWS = ROWS // WIDTH
+VISITS = GROUPS + WINDOWS - 1
 
 sharpness = 4.0
 kinetic_fast = 0.6
@@ -96,9 +101,9 @@
     ext_hbm,
     te_hbm,
     pe_hbm,
-    t2,
-    f2,
-    sens,
+    temp_out,
+    frac_out,
+    sens_out,
     t0p,
     wp,
     t1p,
@@ -109,10 +114,14 @@
     pe,
     tb,
     f1,
+    t2,
+    f2,
+    sens,
     tab,
     rs,
     spread,
     cell,
+    mark,
     loc,
     ploc,
     ext,
@@ -141,10 +150,13 @@
     fmat,
     fv,
     oh_lane,
+    oh_group,
+    row_group,
     column,
     load_sem,
     send_sem,
     recv_sem,
+    out_sem,
 ):
     gx, gy, gz = lax.axis_index("gx"), lax.axis_index("gy"), lax.axis_index("gz")
     zh, c = gz // 2, gz % 2
@@ -180,6 +192,7 @@
             ("dn", dn_hbm, dn),
             ("te", te_hbm, te),
             ("cell", cell_hbm, cell),
+            ("mark", cell_hbm, mark),
             ("loc", loc_hbm, loc),
             ("ext", ext_hbm, ext),
             ("coef", coef_hbm, tab.at[gy, c]),
@@ -232,7 +245,7 @@
     loads["dn"].wait()
     loads["te"].wait()
 
-    @pl.loop(0, NX)
+    @pl.loop(0, NX, unroll=2)
     def _(i):
         wp[i + 1] = dn[i] * te[i]
 
@@ -264,6 +277,7 @@
 
     for name in ("cell", "loc", "ext"):
         loads[name].wait()
+    loads["mark"].wait()
     cell_row = cell[...] >> 8
     oh_lane[...] = one_hot((cell[...] & (NZ - 1)).astype(F32).astype(BF16), column[...], NZ)
     row_c[...] = cell_row
@@ -274,14 +288,59 @@
     for name in ("f0", "st", "pe"):
         loads[name].wait()
 
-    def put(k, rows, x):
+    visits = []
+    group, window = jnp.int32(0), jnp.int32(0)
+    for _ in range(VISITS):
+        over = group >= GROUPS
+        at = jnp.minimum(group, GROUPS - 1)
+        visits.append((at, window, jnp.where(over, -1, window * WIDTH)))
+        last = mark[0, at * GROUP + (GROUP - 1)] >> 8
+        more = jnp.logical_and(last >= (window + 1) * WIDTH, jnp.logical_not(over))
+        window = jnp.where(more, window + 1, window)
+        group = jnp.where(more, group, group + 1)
+
+    for k in range(GROUPS):
+        oh_group[k] = oh_lane[:, k * GROUP : (k + 1) * GROUP]
+        row_group[k] = row_c[:, k * GROUP : (k + 1) * GROUP]
+
+    def put(k, i, x):
         high, low = halves(x)
-        fmat[k, rows, 0:NZ] = high
-        fmat[k, rows, NZ : 2 * NZ] = low
-
-    @pl.loop(0, NX)
+        rows = pl.ds(pl.multiple_of(lax.rem(i, 2) * NY, NY), NY)
+        fmat[i // 2, k, rows, 0:NZ] = high
+        fmat[i // 2, k, rows, NZ : 2 * NZ] = low
+
+    def pick(fields):
+        lo, hi = fields
+        count = hi - lo
+        found = []
+        for at, window, start in visits:
+            hot = oh_group[at]
+            part = jnp.dot(
+                fmat[window, lo:hi].reshape(count * WIDTH, 2 * NZ),
+                jnp.concatenate([hot, hot], axis=0),
+                preferred_element_type=F32,
+            )
+            wanted = jnp.where(start < 0, -1, row_group[at] - start)
+            hit = row_hit(wanted, WIDTH)
+            found.append(
+                [
+                    jnp.sum(
+                        jnp.where(hit, part[f * WIDTH : (f + 1) * WIDTH], 0.0),
+                        axis=0,
+                        keepdims=True,
+                    )
+                    for f in range(count)
+                ]
+            )
+        for k in range(GROUPS):
+            for f in range(count):
+                total = jnp.zeros((1, GROUP), F32)
+                for (at, _, _), values in zip(visits, found):
+                    total = total + jnp.where(at == k, values[f], 0.0)
+                fv[lo + f, :, k * GROUP : (k + 1) * GROUP] = total
+
+    @pl.loop(0, NX, unroll=2)
     def _(i):
-        rows = pl.ds(pl.multiple_of(i * NY, NY), NY)
         t, tw = t0p[i + 1], te[i]
         lifted = t - bath
         growth = rate(st[i]) * (1.0 - f0[i]) * gate(t)
@@ -289,9 +348,9 @@
         f1[i] = new
         tb[i] = enthalpy * growth
         slope = (enthalpy * tw + pe[i]) * (rate(st[i]) * (1.0 - new)) * -sharpness
-        put(0, rows, lifted)
-        put(1, rows, tw * lifted)
-        put(2, rows, slope * lifted)
+        put(0, i, lifted)
+        put(1, i, tw * lifted)
+        put(2, i, slope * lifted)
 
     def gather(matrix, size, hot, row, out):
         found = jnp.dot(
@@ -317,8 +376,7 @@
     def hot_lanes(ref):
         return one_hot(ref[...].astype(BF16), column[...], 256)
 
-    for k in range(3):
-        gather(fmat.at[k], ROWS, oh_lane[...], row_c[...], fv.at[k])
+    pick((0, 3))
 
     loads["coef"].wait()
     for copy in table:
@@ -353,20 +411,18 @@
     for k in range(2):
         zt[k] = z_halo(zr[0, k : k + 1], zr[1, k : k + 1])
 
-    @pl.loop(0, NX)
+    @pl.loop(0, NX, unroll=2)
     def _(i):
         t = t0p[i + 1]
         around = neighbours(t, t0p[i], t0p[i + 2], yr[0, 0, i], yr[1, 0, i], zt[0, i])
         adjoint = neighbours(wp[i + 1], wp[i], wp[i + 2], yr[0, 1, i], yr[1, 1, i], zt[1, i])
         d, tw = dn[i], te[i]
-        rows = pl.ds(pl.multiple_of(i * NY, NY), NY)
         plain = t + d * (around - 6.0 * t) + tb[i]
         tb[i] = plain
-        put(3, rows, plain)
-        put(4, rows, tw * (plain - bath) + (tw * (1.0 - 6.0 * d) + adjoint) * (t - bath))
-
-    for k in range(3, 5):
-        gather(fmat.at[k], ROWS, oh_lane[...], row_c[...], fv.at[k])
+        put(3, i, plain)
+        put(4, i, tw * (plain - bath) + (tw * (1.0 - 6.0 * d) + adjoint) * (t - bath))
+
+    pick((3, 5))
 
     reply.wait_recv()
     drain = ext[...] * (val_a[...] + ret[...])
@@ -376,7 +432,7 @@
     slots = send(sg, psg, 17, partner)
     sink[...] = scatter(val_a[...], ROWS, oh_lane[...], row_c[...])
 
-    @pl.loop(0, NX)
+    @pl.loop(0, NX, unroll=2)
     def _(i):
         rows = pl.ds(pl.multiple_of(i * NY, NY), NY)
         drain = sink[rows, :]
@@ -386,6 +442,8 @@
         f2[i] = f1[i] + growth
         t2[i] = t1 - 6.0 * dn[i] * t1 + enthalpy * growth - drain * (t1 - bath)
 
+    frac_copy = pltpu.make_async_copy(f2, frac_out, out_sem.at[0])
+    frac_copy.start()
     ys1[0] = t1p[1:17, 0:1, :]
     ys1[1] = t1p[1:17, NY - 1 : NY, :]
     left, right = z_faces(t1p[1:17])
@@ -415,31 +473,49 @@
     yr1[1] = jnp.where(gy < 3, yr1[1], 0.0)
     zt[0] = z_halo(zr1[0], zr1[1])
 
-    @pl.loop(0, NX)
+    @pl.loop(0, NX, unroll=4)
     def _(i):
         around = neighbours(
             t1p[i + 1], t1p[i], t1p[i + 2], yr1[0, i], yr1[1, i], zt[0, i]
         )
         t2[i] = t2[i] + dn[i] * around
 
+    temp_copy = pltpu.make_async_copy(t2, temp_out, out_sem.at[1])
+    temp_copy.start()
     total = spread[gy, c]
     for copy, (j, _, _, _) in zip(shares, peers):
         copy.wait_recv()
         total = total + rs[j]
     sens[...] = total
+    sens_copy = pltpu.make_async_copy(sens, sens_out, out_sem.at[2])
+    sens_copy.start()
     for wait in sent:
         wait()
-
-
-def deliver(t2, f2, sens, temp_out, frac_out, sens_out, sem):
-    copies = [
-        pltpu.make_async_copy(source, target, sem.at[k])
-        for k, (source, target) in enumerate(((t2, temp_out), (f2, frac_out), (sens, sens_out)))
+    frac_copy.wait()
+    temp_copy.wait()
+    sens_copy.wait()
+
+
+def deliver(t2, f2, sens, temp_out, frac_out, sens_out, t2v, f2v, sv, read_sem, write_sem):
+    pieces = []
+    for source, middle, target in ((t2, t2v, temp_out), (f2, f2v, frac_out)):
+        for k in range(4):
+            part = pl.ds(4 * k, 4)
+            pieces.append((source.at[part], middle.at[part], target.at[part]))
+    pieces.append((sens, sv, sens_out))
+    reads = [
+        pltpu.make_async_copy(a, b, read_sem.at[k]) for k, (a, b, _) in enumerate(pieces)
     ]
-    for copy in copies:
-        copy.start()
-    for copy in copies:
-        copy.wait()
+    writes = [
+        pltpu.make_async_copy(b, c, write_sem.at[k]) for k, (_, b, c) in enumerate(pieces)
+    ]
+    for read in reads:
+        read.start()
+    for read, write in zip(reads, writes):
+        read.wait()
+        write.start()
+    for write in writes:
+        write.wait()
 
 
 def on_device(t0, f0, dn, st, coef, cell, loc, ext, active, te, pe):
@@ -452,12 +528,14 @@
         [vmem(padded, F32)] * 3
         + [vmem(field, F32)] * 2
         + [vmem(field, I32)]
-        + [vmem(field, F32)] * 4
+        + [vmem(field, F32)] * 6
+        + [vmem((CROWS, 128), F32)]
         + [
             vmem((4, 2, CROWS, 128), F32),
             vmem((8, CROWS, 128), F32),
             vmem((4, 2, CROWS, 128), F32),
             vmem(row, I32),
+            pltpu.SMEM(row, I32),
             vmem(row, I32),
             vmem(row, I32),
             vmem(row, F32),
@@ -474,13 +552,16 @@
             vmem((ROWS, NZ), F32),
             vmem((HROWS, 256), F32),
             vmem((HROWS, 512), BF16),
-            vmem((5, ROWS, 512), BF16),
+            vmem((WINDOWS, 5, WIDTH, 512), BF16),
             vmem((5, 1, SLOTS), F32),
             vmem((NZ, SLOTS), BF16),
+            vmem((GROUPS, NZ, GROUP), BF16),
+            vmem((GROUPS, 1, GROUP), I32),
             vmem((256, 128), BF16),
-            pltpu.SemaphoreType.DMA((10,)),
+            pltpu.SemaphoreType.DMA((11,)),
             pltpu.SemaphoreType.DMA((31,)),
             pltpu.SemaphoreType.DMA((31,)),
+            pltpu.SemaphoreType.DMA((3,)),
         ]
     )
     results = (
@@ -492,7 +573,7 @@
         kernel,
         out_shape=results,
         in_specs=[pl.BlockSpec(memory_space=pltpu.SMEM)] + [anywhere] * 10,
-        out_specs=(pl.BlockSpec(memory_space=vmem),) * 3,
+        out_specs=(anywhere,) * 3,
         scratch_shapes=scratch,
         compiler_params=pltpu.CompilerParams(
             collective_id=0, has_side_effects=True, vmem_limit_bytes=56 * 2**20
@@ -513,9 +594,11 @@
     temp, frac, sens = pl.pallas_call(
         deliver,
         out_shape=results,
-        in_specs=[pl.BlockSpec(memory_space=vmem)] * 3,
+        in_specs=[anywhere] * 3,
         out_specs=(anywhere,) * 3,
-        scratch_shapes=[pltpu.SemaphoreType.DMA((3,))],
+        scratch_shapes=[vmem(field, F32)] * 2
+        + [vmem((CROWS, 128), F32)]
+        + [pltpu.SemaphoreType.DMA((9,))] * 2,
     )(*done)
     return temp, frac, sens.reshape(CHUNK)
 

time: 38.3 us -> 37.4 us (0.977)
  Pallas kernels: 36.9 us -> 36 us
    pallas_call x1, Pallas kernels: 34.7 us -> 33.9 us  [on_device(): pl.pallas_call(kernel, out_shape=results, in_specs=[pl.BlockSpec(memory_s...]
where the time goes in v3:
time: 37.4 us; the launch traced here: 37.3 us
  Pallas kernels  36 us (96%)
  between operations  1.29 us (3%)
    pallas_call x1, Pallas kernels, on_device(): pl.pallas_call(kernel, out_shape=results, in_specs=[pl.BlockSpec(memory_s...  33.9 us
    pallas_call x1, Pallas kernels, on_device(): pl.pallas_call(deliver, out_shape=results, in_specs=[anywhere] * 3, out_s...  2.11 us

profile of v3, /device:TPU:1, one launch (start us, length us, event | category | flops | bytes accessed | tf_op | source)
XLA Modules:
  0.0 37.3 jit_solution(5640393395845263751)
XLA Ops:
  1.3 33.9 %shard_map.130 = (f32[16,32,256]{2,1,0:T(8,128)}, f32[16,32,256]{2,1,0:T(8,128)}, f32[56,128]{1,0:T(8,128)}) custom-call(s32[1]{0:T(128)S(6)} %copy.14.active, f32[16,32,256]{2,1,0:T(8,128)} %t0_hbm.1, f32[16,32,256]{2,1,0:T(8,128)} %f0_hbm.1, f32[16,32,256]{2,1,0:T(8,128)} %dn_hbm.1, s32[16,32,256]{2,1,0:T(8,128)} %st_hbm.1, f32[56,128]{1,0:T(8,128)} %bitcast.5, ...), custom_call_target="tpu_custom_call" | custom-call | tf_op jit(solution)/shard_map/pallas_call | solution.py:572
  35.2 2.1 %shard_map.131 = (f32[16,32,256]{2,1,0:T(8,128)}, f32[16,32,256]{2,1,0:T(8,128)}, f32[56,128]{1,0:T(8,128)}) custom-call(f32[16,32,256]{2,1,0:T(8,128)} %get-tuple-element.9.t2, f32[16,32,256]{2,1,0:T(8,128)} %get-tuple-element.10.f2, f32[56,128]{1,0:T(8,128)} %get-tuple-element.11.sens), custom_call_target="tpu_custom_call" | custom-call | tf_op jit(solution)/shard_map/pallas_call | solution.py:594

commit v4 on v3

--- a/solution.py
+++ b/solution.py
@@ -149,6 +149,7 @@
     tmat,
     fmat,
     fv,
+    pfv,
     oh_lane,
     oh_group,
     row_group,
@@ -166,7 +167,6 @@
     mate = (gx, gy, zh * 2 + (1 - c))
     x_up, x_down = (jnp.minimum(gx + 1, 15), gy, gz), (jnp.maximum(gx - 1, 0), gy, gz)
     has_up, has_down = gx < 15, gx > 0
-    first, second = zh == 0, zh == 1
     y_up, y_down = (gx, lax.rem(gy + 1, 4), gz), (gx, lax.rem(gy + 3, 4), gz)
     peers = []
     for j in range(1, 8):
@@ -178,12 +178,12 @@
     def greet(device):
         pl.semaphore_signal(barrier, inc=1, device_id=device, device_id_type=MESH)
 
-    pl.when(first)(lambda: greet(partner))
+    greet(partner)
     pl.when(has_up)(lambda: greet(x_up))
     pl.when(has_down)(lambda: greet(x_down))
     for _, _, _, device in peers:
         greet(device)
-    expected = 7 + has_up.astype(I32) + has_down.astype(I32) + zh
+    expected = 7 + has_up.astype(I32) + has_down.astype(I32) + 1
 
     loads = {}
     for k, (name, source, target) in enumerate(
@@ -257,23 +257,15 @@
         zs[1, k : k + 1] = jnp.where(even, left, right)
 
     pl.semaphore_wait(barrier, expected)
+    request = send(loc_hbm, ploc, 0, partner)
+    outer = send(zs.at[1], zr.at[1], 8, partner)
     table = [send(coef_hbm, tab.at[gy, c], j, device) for j, _, _, device in peers]
-    request = remote(loc_hbm, ploc, 0, partner)
-    outer = remote(zs.at[1], zr.at[1], 8, partner)
-
-    def ask():
-        request.start()
-        outer.start()
-
-    pl.when(second)(ask)
     halo = [
         send(zs.at[0], zr.at[0], 9, mate),
         send(ys.at[0], yr.at[1], 14, y_down),
         send(ys.at[1], yr.at[0], 15, y_up),
     ]
     halo_x = [send_x(t0p, 10), send_x(wp, 12)]
-    sent.append(request.wait_send)
-    sent.append(outer.wait_send)
 
     for name in ("cell", "loc", "ext"):
         loads[name].wait()
@@ -377,6 +369,15 @@
         return one_hot(ref[...].astype(BF16), column[...], 256)
 
     pick((0, 3))
+    fv[0] = ext[...] * fv[0]
+    fv[1] = ext[...] * (ext[...] * fv[1])
+    fv[2] = ext[...] * fv[2]
+    early = send(fv.at[pl.ds(0, 3)], pfv.at[pl.ds(0, 3)], 17, partner)
+
+    def slot_gradient(value, kept):
+        g = gate(kept[3] - value * kept[0])
+        return 2.0 * value * kept[1] - kept[4] - kept[2] * (g * (1.0 - g))
+
 
     loads["coef"].wait()
     for copy in table:
@@ -387,10 +388,8 @@
     tmat[...] = jnp.concatenate(
         [pieces[0][0], pieces[1][0], pieces[0][1], pieces[1][1]], axis=1
     )
-    gather(tmat, HROWS, hot_lanes(lane_a), row_a[...], val_a)
 
     request.wait_recv()
-    pl.when(first)(ask)
     row, lane = decode(ploc[...], gx, zh)
     row_b[...], lane_b[...] = row, lane.astype(F32)
     gather(tmat, HROWS, hot_lanes(lane_b), row_b[...], val_b)
@@ -423,27 +422,22 @@
         put(4, i, tw * (plain - bath) + (tw * (1.0 - 6.0 * d) + adjoint) * (t - bath))
 
     pick((3, 5))
+    fv[4] = ext[...] * fv[4]
+    late = send(fv.at[pl.ds(3, 2)], pfv.at[pl.ds(3, 2)], 31, partner)
+    gather(tmat, HROWS, hot_lanes(lane_a), row_a[...], val_a)
+
+    sg[...] = slot_gradient(val_a[...], fv)
+    acc[...] = scatter(sg[...], HROWS, hot_lanes(lane_a), row_a[...])
 
     reply.wait_recv()
-    drain = ext[...] * (val_a[...] + ret[...])
-    val_a[...] = drain
-    g = gate(fv[3] - drain * fv[0])
-    sg[...] = -ext[...] * (fv[4] - 2.0 * drain * fv[1] + fv[2] * (g * (1.0 - g)))
-    slots = send(sg, psg, 17, partner)
+    val_a[...] = ext[...] * (val_a[...] + ret[...])
     sink[...] = scatter(val_a[...], ROWS, oh_lane[...], row_c[...])
 
-    @pl.loop(0, NX, unroll=2)
+    @pl.loop(0, NX, unroll=4)
     def _(i):
         rows = pl.ds(pl.multiple_of(i * NY, NY), NY)
-        drain = sink[rows, :]
-        t1 = tb[i] - drain * (t0p[i + 1] - bath)
-        t1p[i + 1] = t1
-        growth = rate(st[i]) * (1.0 - f1[i]) * gate(t1)
-        f2[i] = f1[i] + growth
-        t2[i] = t1 - 6.0 * dn[i] * t1 + enthalpy * growth - drain * (t1 - bath)
-
-    frac_copy = pltpu.make_async_copy(f2, frac_out, out_sem.at[0])
-    frac_copy.start()
+        t1p[i + 1] = tb[i] - sink[rows, :] * (t0p[i + 1] - bath)
+
     ys1[0] = t1p[1:17, 0:1, :]
     ys1[1] = t1p[1:17, NY - 1 : NY, :]
     left, right = z_faces(t1p[1:17])
@@ -456,8 +450,9 @@
         send(ys1.at[1], yr1.at[0], 23, y_up),
     ]
     halo_x = send_x(t1p, 20)
-    acc[...] = scatter(sg[...], HROWS, hot_lanes(lane_a), row_a[...])
-    slots.wait_recv()
+    early.wait_recv()
+    late.wait_recv()
+    psg[...] = slot_gradient(val_b[...], pfv)
     acc[...] += scatter(psg[...], HROWS, hot_lanes(lane_b), row_b[...])
     for g in range(4):
         for part in range(2):
@@ -466,6 +461,17 @@
         send(spread.at[pgy, pc], rs.at[j], 23 + j, device) for j, pgy, pc, device in peers
     ]
 
+    @pl.loop(0, NX, unroll=2)
+    def _(i):
+        rows = pl.ds(pl.multiple_of(i * NY, NY), NY)
+        drain = sink[rows, :]
+        t1 = t1p[i + 1]
+        growth = rate(st[i]) * (1.0 - f1[i]) * gate(t1)
+        f2[i] = f1[i] + growth
+        t2[i] = t1 - 6.0 * dn[i] * t1 + enthalpy * growth - drain * (t1 - bath)
+
+    frac_copy = pltpu.make_async_copy(f2, frac_out, out_sem.at[0])
+    frac_copy.start()
     for copy in halo:
         copy.wait_recv()
     halo_x()
@@ -554,13 +560,14 @@
             vmem((HROWS, 512), BF16),
             vmem((WINDOWS, 5, WIDTH, 512), BF16),
             vmem((5, 1, SLOTS), F32),
+            vmem((5, 1, SLOTS), F32),
             vmem((NZ, SLOTS), BF16),
             vmem((GROUPS, NZ, GROUP), BF16),
             vmem((GROUPS, 1, GROUP), I32),
             vmem((256, 128), BF16),
             pltpu.SemaphoreType.DMA((11,)),
-            pltpu.SemaphoreType.DMA((31,)),
-            pltpu.SemaphoreType.DMA((31,)),
+            pltpu.SemaphoreType.DMA((32,)),
+            pltpu.SemaphoreType.DMA((32,)),
             pltpu.SemaphoreType.DMA((3,)),
         ]
     )

time: 37.4 us -> 33.1 us (0.89)
  Pallas kernels: 36 us -> 31.7 us
    pallas_call x1, Pallas kernels: 33.9 us -> 29.6 us  [on_device(): pl.pallas_call(kernel, out_shape=results, in_specs=[pl.BlockSpec(memory_s...]
where the time goes in v4:
time: 33.1 us; the launch traced here: 33 us
  Pallas kernels  31.7 us (96%)
  between operations  1.29 us (4%)
    pallas_call x1, Pallas kernels, on_device(): pl.pallas_call(kernel, out_shape=results, in_specs=[pl.BlockSpec(memory_s...  29.6 us
    pallas_call x1, Pallas kernels, on_device(): pl.pallas_call(deliver, out_shape=results, in_specs=[anywhere] * 3, out_s...  2.11 us

profile of v4, /device:TPU:1, one launch (start us, length us, event | category | flops | bytes accessed | tf_op | source)
XLA Modules:
  0.0 33.0 jit_solution(16182509138262561033)
XLA Ops:
  1.3 29.6 %shard_map.130 = (f32[16,32,256]{2,1,0:T(8,128)}, f32[16,32,256]{2,1,0:T(8,128)}, f32[56,128]{1,0:T(8,128)}) custom-call(s32[1]{0:T(128)S(6)} %copy.14.active, f32[16,32,256]{2,1,0:T(8,128)} %t0_hbm.1, f32[16,32,256]{2,1,0:T(8,128)} %f0_hbm.1, f32[16,32,256]{2,1,0:T(8,128)} %dn_hbm.1, s32[16,32,256]{2,1,0:T(8,128)} %st_hbm.1, f32[56,128]{1,0:T(8,128)} %bitcast.5, ...), custom_call_target="tpu_custom_call" | custom-call | tf_op jit(solution)/shard_map/pallas_call | solution.py:579
  30.9 2.1 %shard_map.131 = (f32[16,32,256]{2,1,0:T(8,128)}, f32[16,32,256]{2,1,0:T(8,128)}, f32[56,128]{1,0:T(8,128)}) custom-call(f32[16,32,256]{2,1,0:T(8,128)} %get-tuple-element.9.t2, f32[16,32,256]{2,1,0:T(8,128)} %get-tuple-element.10.f2, f32[56,128]{1,0:T(8,128)} %get-tuple-element.11.sens), custom_call_target="tpu_custom_call" | custom-call | tf_op jit(solution)/shard_map/pallas_call | solution.py:601

commit v5 on v4

--- a/solution.py
+++ b/solution.py
@@ -101,9 +101,9 @@
     ext_hbm,
     te_hbm,
     pe_hbm,
-    temp_out,
-    frac_out,
-    sens_out,
+    t2,
+    f2,
+    sens,
     t0p,
     wp,
     t1p,
@@ -114,9 +114,6 @@
     pe,
     tb,
     f1,
-    t2,
-    f2,
-    sens,
     tab,
     rs,
     spread,
@@ -157,7 +154,6 @@
     load_sem,
     send_sem,
     recv_sem,
-    out_sem,
 ):
     gx, gy, gz = lax.axis_index("gx"), lax.axis_index("gy"), lax.axis_index("gz")
     zh, c = gz // 2, gz % 2
@@ -470,8 +466,6 @@
         f2[i] = f1[i] + growth
         t2[i] = t1 - 6.0 * dn[i] * t1 + enthalpy * growth - drain * (t1 - bath)
 
-    frac_copy = pltpu.make_async_copy(f2, frac_out, out_sem.at[0])
-    frac_copy.start()
     for copy in halo:
         copy.wait_recv()
     halo_x()
@@ -486,42 +480,24 @@
         )
         t2[i] = t2[i] + dn[i] * around
 
-    temp_copy = pltpu.make_async_copy(t2, temp_out, out_sem.at[1])
-    temp_copy.start()
     total = spread[gy, c]
     for copy, (j, _, _, _) in zip(shares, peers):
         copy.wait_recv()
         total = total + rs[j]
     sens[...] = total
-    sens_copy = pltpu.make_async_copy(sens, sens_out, out_sem.at[2])
-    sens_copy.start()
     for wait in sent:
         wait()
-    frac_copy.wait()
-    temp_copy.wait()
-    sens_copy.wait()
-
-
-def deliver(t2, f2, sens, temp_out, frac_out, sens_out, t2v, f2v, sv, read_sem, write_sem):
-    pieces = []
-    for source, middle, target in ((t2, t2v, temp_out), (f2, f2v, frac_out)):
-        for k in range(4):
-            part = pl.ds(4 * k, 4)
-            pieces.append((source.at[part], middle.at[part], target.at[part]))
-    pieces.append((sens, sv, sens_out))
-    reads = [
-        pltpu.make_async_copy(a, b, read_sem.at[k]) for k, (a, b, _) in enumerate(pieces)
+
+
+def deliver(t2, f2, sens, temp_out, frac_out, sens_out, sem):
+    copies = [
+        pltpu.make_async_copy(source, target, sem.at[k])
+        for k, (source, target) in enumerate(((t2, temp_out), (f2, frac_out), (sens, sens_out)))
     ]
-    writes = [
-        pltpu.make_async_copy(b, c, write_sem.at[k]) for k, (_, b, c) in enumerate(pieces)
-    ]
-    for read in reads:
-        read.start()
-    for read, write in zip(reads, writes):
-        read.wait()
-        write.start()
-    for write in writes:
-        write.wait()
+    for copy in copies:
+        copy.start()
+    for copy in copies:
+        copy.wait()
 
 
 def on_device(t0, f0, dn, st, coef, cell, loc, ext, active, te, pe):
@@ -534,8 +510,7 @@
         [vmem(padded, F32)] * 3
         + [vmem(field, F32)] * 2
         + [vmem(field, I32)]
-        + [vmem(field, F32)] * 6
-        + [vmem((CROWS, 128), F32)]
+        + [vmem(field, F32)] * 4
         + [
             vmem((4, 2, CROWS, 128), F32),
             vmem((8, CROWS, 128), F32),
@@ -568,7 +543,6 @@
             pltpu.SemaphoreType.DMA((11,)),
             pltpu.SemaphoreType.DMA((32,)),
             pltpu.SemaphoreType.DMA((32,)),
-            pltpu.SemaphoreType.DMA((3,)),
         ]
     )
     results = (
@@ -578,9 +552,9 @@
     )
     done = pl.pallas_call(
         kernel,
-        out_shape=results,
+        out_shape=(vmem(field, F32), vmem(field, F32), vmem((CROWS, 128), F32)),
         in_specs=[pl.BlockSpec(memory_space=pltpu.SMEM)] + [anywhere] * 10,
-        out_specs=(anywhere,) * 3,
+        out_specs=(pl.BlockSpec(memory_space=vmem),) * 3,
         scratch_shapes=scratch,
         compiler_params=pltpu.CompilerParams(
             collective_id=0, has_side_effects=True, vmem_limit_bytes=56 * 2**20
@@ -603,9 +577,8 @@
         out_shape=results,
         in_specs=[anywhere] * 3,
         out_specs=(anywhere,) * 3,
-        scratch_shapes=[vmem(field, F32)] * 2
-        + [vmem((CROWS, 128), F32)]
-        + [pltpu.SemaphoreType.DMA((9,))] * 2,
+        scratch_shapes=[pltpu.SemaphoreType.DMA((3,))],
+        compiler_params=pltpu.CompilerParams(vmem_limit_bytes=2**20),
     )(*done)
     return temp, frac, sens.reshape(CHUNK)
 

time: 33.1 us -> 31.3 us (0.946)
  Pallas kernels: 31.7 us -> 29.9 us
    pallas_call x1, Pallas kernels: 2.11 us -> 1 us  [on_device(): pl.pallas_call(deliver, out_shape=results, in_specs=[anywhere] * 3, out_s...]
    pallas_call x1, Pallas kernels: 29.6 us -> 28.9 us  [on_device(): pl.pallas_call(kernel, out_shape=(vmem(field, F32), vmem(field, F32), vme...]
where the time goes in v5:
time: 31.3 us; the launch traced here: 31.2 us
  Pallas kernels  29.9 us (96%)
  between operations  1.29 us (4%)
    pallas_call x1, Pallas kernels, on_device(): pl.pallas_call(kernel, out_shape=(vmem(field, F32), vmem(field, F32), vme...  28.9 us
    pallas_call x1, Pallas kernels, on_device(): pl.pallas_call(deliver, out_shape=results, in_specs=[anywhere] * 3, out_s...  1 us

profile of v5, /device:TPU:1, one launch (start us, length us, event | category | flops | bytes accessed | tf_op | source)
XLA Modules:
  0.0 31.2 jit_solution(5356934668232143106)
XLA Ops:
  1.3 28.9 %shard_map.130 = (f32[16,32,256]{2,1,0:T(8,128)S(1)}, f32[16,32,256]{2,1,0:T(8,128)S(1)}, f32[56,128]{1,0:T(8,128)S(1)}) custom-call(s32[1]{0:T(128)S(6)} %copy.14.active, f32[16,32,256]{2,1,0:T(8,128)} %t0_hbm.1, f32[16,32,256]{2,1,0:T(8,128)} %f0_hbm.1, f32[16,32,256]{2,1,0:T(8,128)} %dn_hbm.1, s32[16,32,256]{2,1,0:T(8,128)} %st_hbm.1, f32[56,128]{1,0:T(8,128)} %bitcast.5, ...), custom_call_target="tpu_custom_call" | custom-call | tf_op jit(solution)/shard_map/pallas_call | solution.py:553
  30.2 1.0 %shard_map.131 = (f32[16,32,256]{2,1,0:T(8,128)}, f32[16,32,256]{2,1,0:T(8,128)}, f32[56,128]{1,0:T(8,128)}) custom-call(f32[16,32,256]{2,1,0:T(8,128)S(1)} %get-tuple-element.9.t2, f32[16,32,256]{2,1,0:T(8,128)S(1)} %get-tuple-element.10.f2, f32[56,128]{1,0:T(8,128)S(1)} %get-tuple-element.11.sens), custom_call_target="tpu_custom_call" | custom-call | tf_op jit(solution)/shard_map/pallas_call | solution.py:575

commit v6 on v5

--- a/solution.py
+++ b/solution.py
@@ -24,6 +24,9 @@
 WIDTH = 64
 WINDOWS = ROWS // WIDTH
 VISITS = GROUPS + WINDOWS - 1
+TALL = 128
+TALL_WINDOWS = ROWS // TALL
+TALL_VISITS = GROUPS + TALL_WINDOWS - 1
 
 sharpness = 4.0
 kinetic_fast = 0.6
@@ -90,7 +93,7 @@
 
 
 def kernel(
-    active,
+    live_hbm,
     t0_hbm,
     f0_hbm,
     dn_hbm,
@@ -117,6 +120,7 @@
     tab,
     rs,
     spread,
+    active,
     cell,
     mark,
     loc,
@@ -147,6 +151,11 @@
     fmat,
     fv,
     pfv,
+    hot_a,
+    hot_b,
+    left_b,
+    rises,
+    slopes,
     oh_lane,
     oh_group,
     row_group,
@@ -165,7 +174,7 @@
     has_up, has_down = gx < 15, gx > 0
     y_up, y_down = (gx, lax.rem(gy + 1, 4), gz), (gx, lax.rem(gy + 3, 4), gz)
     peers = []
-    for j in range(1, 8):
+    for j in (4, 5, 2, 3, 6, 7, 1):
         pgy, pc = lax.rem(gy + j // 2, 4), lax.rem(c + j % 2, 2)
         peers.append((j, pgy, pc, (gx, pgy, zh * 2 + pc)))
 
@@ -189,6 +198,7 @@
             ("te", te_hbm, te),
             ("cell", cell_hbm, cell),
             ("mark", cell_hbm, mark),
+            ("active", live_hbm, active),
             ("loc", loc_hbm, loc),
             ("ext", ext_hbm, ext),
             ("coef", coef_hbm, tab.at[gy, c]),
@@ -266,6 +276,7 @@
     for name in ("cell", "loc", "ext"):
         loads[name].wait()
     loads["mark"].wait()
+    loads["active"].wait()
     cell_row = cell[...] >> 8
     oh_lane[...] = one_hot((cell[...] & (NZ - 1)).astype(F32).astype(BF16), column[...], NZ)
     row_c[...] = cell_row
@@ -276,20 +287,31 @@
     for name in ("f0", "st", "pe"):
         loads[name].wait()
 
-    visits = []
-    group, window = jnp.int32(0), jnp.int32(0)
-    for _ in range(VISITS):
-        over = group >= GROUPS
-        at = jnp.minimum(group, GROUPS - 1)
-        visits.append((at, window, jnp.where(over, -1, window * WIDTH)))
-        last = mark[0, at * GROUP + (GROUP - 1)] >> 8
-        more = jnp.logical_and(last >= (window + 1) * WIDTH, jnp.logical_not(over))
-        window = jnp.where(more, window + 1, window)
-        group = jnp.where(more, group, group + 1)
+    def path(count, width):
+        visits = []
+        group, window = jnp.int32(0), jnp.int32(0)
+        for _ in range(count):
+            over = group >= GROUPS
+            at = jnp.minimum(group, GROUPS - 1)
+            visits.append((at, window, jnp.where(over, -1, window * width)))
+            last = mark[0, at * GROUP + (GROUP - 1)] >> 8
+            more = jnp.logical_and(last >= (window + 1) * width, jnp.logical_not(over))
+            window = jnp.where(more, window + 1, window)
+            group = jnp.where(more, group, group + 1)
+        return visits
+
+    visits, tall = path(VISITS, WIDTH), path(TALL_VISITS, TALL)
 
     for k in range(GROUPS):
         oh_group[k] = oh_lane[:, k * GROUP : (k + 1) * GROUP]
         row_group[k] = row_c[:, k * GROUP : (k + 1) * GROUP]
+
+    ends = [jnp.int32(TALL_VISITS)] * TALL_WINDOWS
+    for k, (at, window, start) in enumerate(tall):
+        wanted = jnp.where(start < 0, -1, row_group[at] - start)
+        rises[k] = jnp.where(row_hit(wanted, TALL), 1.0, 0.0).astype(BF16)
+        ends = [jnp.where(window == w, k, end) for w, end in enumerate(ends)]
+    sink[TALL_VISITS] = jnp.zeros((TALL, NZ), F32)
 
     def put(k, i, x):
         high, low = halves(x)
@@ -347,19 +369,21 @@
         found = jnp.where(row_hit(row, size), found, 0.0)
         out[...] = jnp.sum(found, axis=0, keepdims=True)
 
-    def scatter(value, size, hot, row):
+    def scatter(value, hot, left):
         high, low = halves(value)
         right = jnp.concatenate(
             [hot * jnp.broadcast_to(high, hot.shape), hot * jnp.broadcast_to(low, hot.shape)],
             axis=1,
         )
-        left = jnp.where(row_hit(row, size), 1.0, 0.0).astype(BF16)
         return lax.dot_general(
             jnp.concatenate([left, left], axis=1),
             right,
             (((1,), (1,)), ((), ())),
             preferred_element_type=F32,
         )
+
+    def row_marks(ref):
+        return jnp.where(row_hit(ref[...], HROWS), 1.0, 0.0).astype(BF16)
 
     def hot_lanes(ref):
         return one_hot(ref[...].astype(BF16), column[...], 256)
@@ -388,7 +412,8 @@
     request.wait_recv()
     row, lane = decode(ploc[...], gx, zh)
     row_b[...], lane_b[...] = row, lane.astype(F32)
-    gather(tmat, HROWS, hot_lanes(lane_b), row_b[...], val_b)
+    hot_b[...] = hot_lanes(lane_b)
+    gather(tmat, HROWS, hot_b[...], row_b[...], val_b)
     reply = send(val_b, ret, 16, partner)
 
     for copy in halo:
@@ -420,19 +445,41 @@
     pick((3, 5))
     fv[4] = ext[...] * fv[4]
     late = send(fv.at[pl.ds(3, 2)], pfv.at[pl.ds(3, 2)], 31, partner)
-    gather(tmat, HROWS, hot_lanes(lane_a), row_a[...], val_a)
+    hot_a[...] = hot_lanes(lane_a)
+    gather(tmat, HROWS, hot_a[...], row_a[...], val_a)
 
     sg[...] = slot_gradient(val_a[...], fv)
-    acc[...] = scatter(sg[...], HROWS, hot_lanes(lane_a), row_a[...])
+    acc[...] = scatter(sg[...], hot_a[...], row_marks(row_a))
+    left_b[...] = row_marks(row_b)
 
     reply.wait_recv()
     val_a[...] = ext[...] * (val_a[...] + ret[...])
-    sink[...] = scatter(val_a[...], ROWS, oh_lane[...], row_c[...])
-
-    @pl.loop(0, NX, unroll=4)
-    def _(i):
-        rows = pl.ds(pl.multiple_of(i * NY, NY), NY)
-        t1p[i + 1] = tb[i] - sink[rows, :] * (t0p[i + 1] - bath)
+    high, low = halves(val_a[...])
+    for k in range(GROUPS):
+        cols = slice(k * GROUP, (k + 1) * GROUP)
+        hot = oh_group[k]
+        slopes[k, :, 0:GROUP] = hot * jnp.broadcast_to(high[:, cols], hot.shape)
+        slopes[k, :, GROUP : 2 * GROUP] = hot * jnp.broadcast_to(low[:, cols], hot.shape)
+    running = None
+    for k, (at, window, _) in enumerate(tall):
+        rise = rises[k]
+        part = lax.dot_general(
+            jnp.concatenate([rise, rise], axis=1),
+            slopes[at],
+            (((1,), (1,)), ((), ())),
+            preferred_element_type=F32,
+        )
+        if k:
+            part = part + jnp.where(window == tall[k - 1][1], running, 0.0)
+        sink[k] = part
+        running = part
+
+    per = TALL // NY
+    for w, end in enumerate(ends):
+        for k in range(per):
+            i = w * per + k
+            drain = sink[end, k * NY : (k + 1) * NY, :]
+            t1p[i + 1] = tb[i] - drain * (t0p[i + 1] - bath)
 
     ys1[0] = t1p[1:17, 0:1, :]
     ys1[1] = t1p[1:17, NY - 1 : NY, :]
@@ -449,7 +496,7 @@
     early.wait_recv()
     late.wait_recv()
     psg[...] = slot_gradient(val_b[...], pfv)
-    acc[...] += scatter(psg[...], HROWS, hot_lanes(lane_b), row_b[...])
+    acc[...] += scatter(psg[...], hot_b[...], left_b[...])
     for g in range(4):
         for part in range(2):
             spread[g, part] = acc[g * CROWS : (g + 1) * CROWS, part * 128 : (part + 1) * 128]
@@ -457,21 +504,23 @@
         send(spread.at[pgy, pc], rs.at[j], 23 + j, device) for j, pgy, pc, device in peers
     ]
 
-    @pl.loop(0, NX, unroll=2)
-    def _(i):
-        rows = pl.ds(pl.multiple_of(i * NY, NY), NY)
-        drain = sink[rows, :]
-        t1 = t1p[i + 1]
-        growth = rate(st[i]) * (1.0 - f1[i]) * gate(t1)
-        f2[i] = f1[i] + growth
-        t2[i] = t1 - 6.0 * dn[i] * t1 + enthalpy * growth - drain * (t1 - bath)
-
-    for copy in halo:
+    for w, end in enumerate(ends):
+
+        @pl.loop(0, per, unroll=2)
+        def _(k):
+            i = w * per + k
+            drain = sink[end, pl.ds(pl.multiple_of(k * NY, NY), NY), :]
+            t1 = t1p[i + 1]
+            growth = rate(st[i]) * (1.0 - f1[i]) * gate(t1)
+            f2[i] = f1[i] + growth
+            t2[i] = t1 - 6.0 * dn[i] * t1 + enthalpy * growth - drain * (t1 - bath)
+
+    for copy in halo[1:]:
         copy.wait_recv()
     halo_x()
     yr1[0] = jnp.where(gy > 0, yr1[0], 0.0)
     yr1[1] = jnp.where(gy < 3, yr1[1], 0.0)
-    zt[0] = z_halo(zr1[0], zr1[1])
+    zt[0] = z_halo(zr1[0], jnp.zeros((1, ROWS), F32))
 
     @pl.loop(0, NX, unroll=4)
     def _(i):
@@ -479,6 +528,12 @@
             t1p[i + 1], t1p[i], t1p[i + 2], yr1[0, i], yr1[1, i], zt[0, i]
         )
         t2[i] = t2[i] + dn[i] * around
+
+    halo[0].wait_recv()
+    outside = jnp.where(outer_live, zr1[1], 0.0)
+    outside = z_block(jnp.where(even, outside, 0.0), jnp.where(even, 0.0, outside))
+    tile = pl.ds(pl.multiple_of((1 - even.astype(I32)) * 128, 128), 128)
+    t2[:, :, tile] = t2[:, :, tile] + dn[:, :, tile] * outside
 
     total = spread[gy, c]
     for copy, (j, _, _, _) in zip(shares, peers):
@@ -515,6 +570,7 @@
             vmem((4, 2, CROWS, 128), F32),
             vmem((8, CROWS, 128), F32),
             vmem((4, 2, CROWS, 128), F32),
+            pltpu.SMEM((1,), I32),
             vmem(row, I32),
             pltpu.SMEM(row, I32),
             vmem(row, I32),
@@ -530,17 +586,22 @@
         + [vmem((2, 1, ROWS), F32)] * 2
         + [
             vmem((2, NX, NY, 128), F32),
-            vmem((ROWS, NZ), F32),
+            vmem((TALL_VISITS + 1, TALL, NZ), F32),
             vmem((HROWS, 256), F32),
             vmem((HROWS, 512), BF16),
             vmem((WINDOWS, 5, WIDTH, 512), BF16),
             vmem((5, 1, SLOTS), F32),
             vmem((5, 1, SLOTS), F32),
+            vmem((256, SLOTS), BF16),
+            vmem((256, SLOTS), BF16),
+            vmem((HROWS, SLOTS), BF16),
+            vmem((TALL_VISITS, TALL, GROUP), BF16),
+            vmem((GROUPS, NZ, 2 * GROUP), BF16),
             vmem((NZ, SLOTS), BF16),
             vmem((GROUPS, NZ, GROUP), BF16),
             vmem((GROUPS, 1, GROUP), I32),
             vmem((256, 128), BF16),
-            pltpu.SemaphoreType.DMA((11,)),
+            pltpu.SemaphoreType.DMA((12,)),
             pltpu.SemaphoreType.DMA((32,)),
             pltpu.SemaphoreType.DMA((32,)),
         ]
@@ -553,7 +614,7 @@
     done = pl.pallas_call(
         kernel,
         out_shape=(vmem(field, F32), vmem(field, F32), vmem((CROWS, 128), F32)),
-        in_specs=[pl.BlockSpec(memory_space=pltpu.SMEM)] + [anywhere] * 10,
+        in_specs=[anywhere] * 11,
         out_specs=(pl.BlockSpec(memory_space=vmem),) * 3,
         scratch_shapes=scratch,
         compiler_params=pltpu.CompilerParams(

time: 31.3 us -> 30.6 us (0.978)
  Pallas kernels: 29.9 us -> 29.2 us
    pallas_call x1, Pallas kernels: 28.9 us -> 28.2 us  [on_device(): pl.pallas_call(kernel, out_shape=(vmem(field, F32), vmem(field, F32), vme...]
where the time goes in v6:
time: 30.6 us; the launch traced here: 30.5 us
  Pallas kernels  29.2 us (95%)
  between operations  1.29 us (4%)
    pallas_call x1, Pallas kernels, on_device(): pl.pallas_call(kernel, out_shape=(vmem(field, F32), vmem(field, F32), vme...  28.2 us
    pallas_call x1, Pallas kernels, on_device(): pl.pallas_call(deliver, out_shape=results, in_specs=[anywhere] * 3, out_s...  1 us

profile of v6, /device:TPU:1, one launch (start us, length us, event | category | flops | bytes accessed | tf_op | source)
XLA Modules:
  0.0 30.5 jit_solution(2487880573783882065)
XLA Ops:
  1.3 28.2 %shard_map.130 = (f32[16,32,256]{2,1,0:T(8,128)S(1)}, f32[16,32,256]{2,1,0:T(8,128)S(1)}, f32[56,128]{1,0:T(8,128)S(1)}) custom-call(s32[1]{0:T(128)S(6)} %copy.14.live_hbm, f32[16,32,256]{2,1,0:T(8,128)} %t0_hbm.1, f32[16,32,256]{2,1,0:T(8,128)} %f0_hbm.1, f32[16,32,256]{2,1,0:T(8,128)} %dn_hbm.1, s32[16,32,256]{2,1,0:T(8,128)} %st_hbm.1, ...), custom_call_target="tpu_custom_call" | custom-call | tf_op jit(solution)/shard_map/pallas_call | solution.py:614
  29.5 1.0 %shard_map.131 = (f32[16,32,256]{2,1,0:T(8,128)}, f32[16,32,256]{2,1,0:T(8,128)}, f32[56,128]{1,0:T(8,128)}) custom-call(f32[16,32,256]{2,1,0:T(8,128)S(1)} %get-tuple-element.9.t2, f32[16,32,256]{2,1,0:T(8,128)S(1)} %get-tuple-element.10.f2, f32[56,128]{1,0:T(8,128)S(1)} %get-tuple-element.11.sens), custom_call_target="tpu_custom_call" | custom-call | tf_op jit(solution)/shard_map/pallas_call | solution.py:636

commit v7 on v6

--- a/solution.py
+++ b/solution.py
@@ -120,6 +120,8 @@
     tab,
     rs,
     spread,
+    theirs,
+    mine,
     active,
     cell,
     mark,
@@ -499,10 +501,14 @@
     acc[...] += scatter(psg[...], hot_b[...], left_b[...])
     for g in range(4):
         for part in range(2):
-            spread[g, part] = acc[g * CROWS : (g + 1) * CROWS, part * 128 : (part + 1) * 128]
-    shares = [
-        send(spread.at[pgy, pc], rs.at[j], 23 + j, device) for j, pgy, pc, device in peers
-    ]
+            spread[part, g] = acc[g * CROWS : (g + 1) * CROWS, part * 128 : (part + 1) * 128]
+    swap = send(spread.at[1 - c], theirs, 24, mate)
+    swap.wait_recv()
+    mine[...] = spread[c] + theirs[...]
+    shares = []
+    for k, far in enumerate((2, 1, 3)):
+        to = lax.rem(gy + far, 4)
+        shares.append((send(mine.at[to], rs.at[k], 25 + k, (gx, to, gz)), k))
 
     for w, end in enumerate(ends):
 
@@ -535,10 +541,10 @@
     tile = pl.ds(pl.multiple_of((1 - even.astype(I32)) * 128, 128), 128)
     t2[:, :, tile] = t2[:, :, tile] + dn[:, :, tile] * outside
 
-    total = spread[gy, c]
-    for copy, (j, _, _, _) in zip(shares, peers):
+    total = mine[gy]
+    for copy, k in shares:
         copy.wait_recv()
-        total = total + rs[j]
+        total = total + rs[k]
     sens[...] = total
     for wait in sent:
         wait()
@@ -568,8 +574,10 @@
         + [vmem(field, F32)] * 4
         + [
             vmem((4, 2, CROWS, 128), F32),
-            vmem((8, CROWS, 128), F32),
-            vmem((4, 2, CROWS, 128), F32),
+            vmem((3, CROWS, 128), F32),
+            vmem((2, 4, CROWS, 128), F32),
+            vmem((4, CROWS, 128), F32),
+            vmem((4, CROWS, 128), F32),
             pltpu.SMEM((1,), I32),
             vmem(row, I32),
             pltpu.SMEM(row, I32),

time: 30.6 us -> 29.8 us (0.974)
  Pallas kernels: 29.2 us -> 28.4 us
    pallas_call x1, Pallas kernels: 28.2 us -> 27.4 us  [on_device(): pl.pallas_call(kernel, out_shape=(vmem(field, F32), vmem(field, F32), vme...]
where the time goes in v7:
time: 29.8 us; the launch traced here: 29.7 us
  Pallas kernels  28.4 us (95%)
  between operations  1.29 us (4%)
    pallas_call x1, Pallas kernels, on_device(): pl.pallas_call(kernel, out_shape=(vmem(field, F32), vmem(field, F32), vme...  27.4 us
    pallas_call x1, Pallas kernels, on_device(): pl.pallas_call(deliver, out_shape=results, in_specs=[anywhere] * 3, out_s...  1 us

profile of v7, /device:TPU:1, one launch (start us, length us, event | category | flops | bytes accessed | tf_op | source)
XLA Modules:
  0.0 29.7 jit_solution(18025504686229094402)
XLA Ops:
  1.3 27.4 %shard_map.130 = (f32[16,32,256]{2,1,0:T(8,128)S(1)}, f32[16,32,256]{2,1,0:T(8,128)S(1)}, f32[56,128]{1,0:T(8,128)S(1)}) custom-call(s32[1]{0:T(128)S(6)} %copy.14.live_hbm, f32[16,32,256]{2,1,0:T(8,128)} %t0_hbm.1, f32[16,32,256]{2,1,0:T(8,128)} %f0_hbm.1, f32[16,32,256]{2,1,0:T(8,128)} %dn_hbm.1, s32[16,32,256]{2,1,0:T(8,128)} %st_hbm.1, ...), custom_call_target="tpu_custom_call" | custom-call | tf_op jit(solution)/shard_map/pallas_call | solution.py:622
  28.7 1.0 %shard_map.131 = (f32[16,32,256]{2,1,0:T(8,128)}, f32[16,32,256]{2,1,0:T(8,128)}, f32[56,128]{1,0:T(8,128)}) custom-call(f32[16,32,256]{2,1,0:T(8,128)S(1)} %get-tuple-element.9.t2, f32[16,32,256]{2,1,0:T(8,128)S(1)} %get-tuple-element.10.f2, f32[56,128]{1,0:T(8,128)S(1)} %get-tuple-element.11.sens), custom_call_target="tpu_custom_call" | custom-call | tf_op jit(solution)/shard_map/pallas_call | solution.py:644

commit v8 on v7

--- a/solution.py
+++ b/solution.py
@@ -267,7 +267,11 @@
     pl.semaphore_wait(barrier, expected)
     request = send(loc_hbm, ploc, 0, partner)
     outer = send(zs.at[1], zr.at[1], 8, partner)
-    table = [send(coef_hbm, tab.at[gy, c], j, device) for j, _, _, device in peers]
+    table = {
+        j: send(coef_hbm, tab.at[gy, c], j, device)
+        for j, _, _, device in peers
+        if j % 2 == 0 or j == 1
+    }
     halo = [
         send(zs.at[0], zr.at[0], 9, mate),
         send(ys.at[0], yr.at[1], 14, y_down),
@@ -402,7 +406,12 @@
 
 
     loads["coef"].wait()
-    for copy in table:
+    passed = [table[1]]
+    for j in (2, 6, 4):
+        table[j].wait_recv()
+        chunk = tab.at[lax.rem(gy + 4 - j // 2, 4), c]
+        passed.append(send(chunk, chunk, j + 1, mate))
+    for copy in passed:
         copy.wait_recv()
     pieces = []
     for part in range(2):

time: 29.8 us -> 29.8 us (level)
  no operation moved by 1% of the time
where the time goes in v8:
time: 29.8 us; the launch traced here: 29.7 us
  Pallas kernels  28.4 us (95%)
  between operations  1.29 us (4%)
    pallas_call x1, Pallas kernels, on_device(): pl.pallas_call(kernel, out_shape=(vmem(field, F32), vmem(field, F32), vme...  27.4 us
    pallas_call x1, Pallas kernels, on_device(): pl.pallas_call(deliver, out_shape=results, in_specs=[anywhere] * 3, out_s...  1 us

profile of v8, /device:TPU:1, one launch (start us, length us, event | category | flops | bytes accessed | tf_op | source)
XLA Modules:
  0.0 29.7 jit_solution(11004618885673663382)
XLA Ops:
  1.3 27.4 %shard_map.130 = (f32[16,32,256]{2,1,0:T(8,128)S(1)}, f32[16,32,256]{2,1,0:T(8,128)S(1)}, f32[56,128]{1,0:T(8,128)S(1)}) custom-call(s32[1]{0:T(128)S(6)} %copy.14.live_hbm, f32[16,32,256]{2,1,0:T(8,128)} %t0_hbm.1, f32[16,32,256]{2,1,0:T(8,128)} %f0_hbm.1, f32[16,32,256]{2,1,0:T(8,128)} %dn_hbm.1, s32[16,32,256]{2,1,0:T(8,128)} %st_hbm.1, ...), custom_call_target="tpu_custom_call" | custom-call | tf_op jit(solution)/shard_map/pallas_call | solution.py:631
  28.7 1.0 %shard_map.131 = (f32[16,32,256]{2,1,0:T(8,128)}, f32[16,32,256]{2,1,0:T(8,128)}, f32[56,128]{1,0:T(8,128)}) custom-call(f32[16,32,256]{2,1,0:T(8,128)S(1)} %get-tuple-element.9.t2, f32[16,32,256]{2,1,0:T(8,128)S(1)} %get-tuple-element.10.f2, f32[56,128]{1,0:T(8,128)S(1)} %get-tuple-element.11.sens), custom_call_target="tpu_custom_call" | custom-call | tf_op jit(solution)/shard_map/pallas_call | solution.py:653
